TPU v7x, 32 devices: a whole 2x2x4 slice. The times are simulated.
32 devices in a mesh: group: 4 (over x, core), replica: 8 (over z, y).
Axes of the slice: x: 2, y: 2, z: 4, core: 2. Of those that a mesh axis runs over, the one named last changes fastest.
Arguments:
- tokens: bfloat16 [16, 1024, 384], P('replica', 'group'), may hold values from -6 to 6
- cotangent: bfloat16 [16, 1024, 384], P('replica', 'group'), may hold values from -6 to 6
- weight: float32 [1774592], P('group'), may hold values from -1.6329932 to 1.6329932
- momentum: float32 [1774592], P('group'), may hold values from -40 to 40
- average: float32 [1774592], P('group'), may hold values from -1.6329932 to 1.6329932
- rate: float32 [1], replicated, may hold values from 0.00015625 to 0.000625
- step: int32 [1], replicated, may hold values from 1 to 20
Outputs:
- output: bfloat16 [16, 1024, 384], P('replica', 'group')
- grad_tokens: bfloat16 [16, 1024, 384], P('replica', 'group')
- grad: float32 [1774592], P('group')
- momentum_new: float32 [1774592], P('group')
- average_new: float32 [1774592], P('group')
- weight_new: float32 [1774592], P('group')
- weight_copy: bfloat16 [1774592], P('group')
All inputs are finite; a program needn't handle non-finite values.
Results may differ from a plain program's by a relative error of at most 0.013.
The roundings to bfloat16 on the way count: a program that leaves them out, or rounds other values in their place, can miss the bound.
Values may be sent and summed in bfloat16 or wider, within the bound.
No kernel may reach another device: no remote copies, remote signals or barrier semaphores. Data moves between devices by JAX's collectives and lax.ppermute only.
A program may use at most 448 MiB of HBM per device.

v0:
```python
from functools import partial

import jax
import jax.numpy as jnp
from jax import lax
from jax.sharding import PartitionSpec as P

D = 384
H = 6
DH = 64
FF = 1536


EPSILON = 1e-06
MOMENT = 0.9
DECAY_MAX = 0.999
INV_ROOT_TWO = 0.7071067811865476
INV_ROOT_TAU = 0.3989422804014327


def split_params(flat_vec):
    layout = (
        (D * 3 * D, (D, 3 * D)),
        (D * D, (D, D)),
        (D * FF, (D, FF)),
        (FF * D, (FF, D)),
        (D, (D,)),
        (D, (D,)),
        (3 * D, (3 * D,)),
        (DH, (DH,)),
        (DH, (DH,)),
        (D, (D,)),
        (D, (D,)),
        (D, (D,)),
        (FF, (FF,)),
        (D, (D,)),
    )
    pieces = []
    offset = 0
    for seg_len, seg_shape in layout:
        pieces.append(flat_vec[offset : offset + seg_len].reshape(seg_shape))
        offset = offset + seg_len
    return tuple(pieces)


def norm_forward(values, scale, shift):
    center = values - jnp.mean(values, -1, keepdims=True)
    inv_std = lax.rsqrt(jnp.mean(center * center, -1, keepdims=True) + EPSILON)
    normed = center * inv_std
    return (normed * scale + shift, normed, inv_std)


def norm_backward(grad_out, normed, inv_std, scale):
    grad_norm = grad_out * scale
    inner = jnp.mean(grad_norm * normed, -1, keepdims=True)
    return inv_std * (grad_norm - jnp.mean(grad_norm, -1, keepdims=True) - normed * inner)


def gelu_slope(values):
    return (
        0.5 * (1.0 + lax.erf(values * INV_ROOT_TWO))
        + values * jnp.exp(-0.5 * values * values) * INV_ROOT_TAU
    )


def cross_dot(left, right):
    return lax.dot_general(
        left, right, (((0,), (0,)), ((), ())), preferred_element_type=jnp.float32
    )


def back_dot(left, right):
    return lax.dot_general(
        left, right, (((1,), (1,)), ((), ())), preferred_element_type=jnp.float32
    )


def head_scores(query_b, key_block_rows, row_mask_values, scale_factor):
    query_masked = query_b * row_mask_values
    scores = (
        jnp.einsum("xuc,xlc->xul", query_masked, key_block_rows, preferred_element_type=jnp.float32)
        * scale_factor
    )
    return (query_masked, scores)


def attend_block(operands, masks, scale_factor):
    query_b, key_block_rows, value_block_rows = operands

    def attend_one_head(total, row_mask_values):
        query_masked, scores = head_scores(query_b, key_block_rows, row_mask_values, scale_factor)
        row_peak = jnp.max(scores, -1, keepdims=True)
        raised = jnp.exp(scores - row_peak)
        row_total = jnp.sum(raised, -1, keepdims=True)
        attention_weights = (raised / row_total).astype(jnp.bfloat16)
        part_out = jnp.einsum(
            "cxu,cuw->cxw",
            attention_weights,
            value_block_rows * row_mask_values,
            preferred_element_type=jnp.float32,
        )
        return (total + part_out, (row_peak + jnp.log(row_total))[..., 0])

    start = jnp.zeros(query_b.shape, jnp.float32)
    return lax.scan(attend_one_head, start, masks)


def head_grads(
    query_b, key_block_rows, value_block_rows, grad_b, log_h, inner_h, row_mask_values, scale_factor
):
    query_masked, scores = head_scores(query_b, key_block_rows, row_mask_values, scale_factor)
    probs = jnp.exp(scores - log_h[..., None])
    gradient_masked = grad_b * row_mask_values
    grad_probs = jnp.einsum(
        "xuc,xlc->xul", gradient_masked, value_block_rows, preferred_element_type=jnp.float32
    )
    inner_h = jnp.sum(probs * grad_probs, -1)
    score_gradient = (probs * (grad_probs - inner_h[..., None])).astype(jnp.bfloat16)
    return (probs, score_gradient, inner_h, query_masked, gradient_masked)


def local_back(operands, masks, scale_factor):
    query_b, key_block_rows, value_block_rows, grad_b, log_b = operands

    def local_one_head(carry, head_in):
        row_mask_values, log_h = head_in
        probs, score_gradient, inner_h, query_masked, gradient_masked = head_grads(
            query_b,
            key_block_rows,
            value_block_rows,
            grad_b,
            log_h,
            None,
            row_mask_values,
            scale_factor,
        )
        grad_query = (
            jnp.einsum(
                "cxu,cuw->cxw",
                score_gradient,
                key_block_rows * row_mask_values,
                preferred_element_type=jnp.float32,
            )
            * scale_factor
        )
        grad_key = (
            jnp.einsum(
                "fji,fjp->fip", score_gradient, query_masked, preferred_element_type=jnp.float32
            )
            * scale_factor
        )
        grad_value = jnp.einsum(
            "fji,fjp->fip",
            probs.astype(jnp.bfloat16),
            gradient_masked,
            preferred_element_type=jnp.float32,
        )
        return ((carry[0] + grad_query, carry[1] + grad_key, carry[2] + grad_value), None)

    start = (
        jnp.zeros(query_b.shape, jnp.float32),
        jnp.zeros(key_block_rows.shape, jnp.float32),
        jnp.zeros(key_block_rows.shape, jnp.float32),
    )
    totals, unused = lax.scan(local_one_head, start, (masks, log_b))
    return totals


def per_device(tokens, cotangent, weight, momentum, average, rate, step):
    image_count, own_len, width = tokens.shape
    row_count = image_count * own_len
    scale_factor = DH ** (-0.5)
    pair_size = 2
    head_masks = (
        lax.broadcasted_iota(jnp.int32, (H, width), 1) // DH
        == lax.broadcasted_iota(jnp.int32, (H, width), 0)
    ).astype(jnp.bfloat16)

    def in_blocks(array):
        return array.reshape((image_count // pair_size, pair_size) + array.shape[1:])

    def unblock(array):
        return array.reshape((image_count,) + array.shape[2:])

    shard_low = weight.astype(jnp.bfloat16)
    gathered = lax.all_gather(shard_low, "group", axis=0, tiled=True)
    (
        w_qkv,
        w_out,
        w_fc1,
        w_fc2,
        g_one,
        b_one,
        b_qkv,
        g_query,
        g_key,
        b_out,
        g_two,
        b_two,
        b_fc1,
        b_fc2,
    ) = split_params(gathered)
    (
        gain_one,
        bias_one,
        bias_qkv,
        gain_query,
        gain_key,
        bias_out,
        gain_two,
        bias_two,
        bias_fc1,
        bias_fc2,
    ) = tuple(
        (
            member.astype(jnp.float32)
            for member in (g_one, b_one, b_qkv, g_query, g_key, b_out, g_two, b_two, b_fc1, b_fc2)
        )
    )
    resid_in = tokens.astype(jnp.float32).reshape(row_count, width)
    ln_one_out, normed_one, inv_one = norm_forward(resid_in, gain_one, bias_one)
    act_one = ln_one_out.astype(jnp.bfloat16)
    qkv_full = jnp.dot(act_one, w_qkv, preferred_element_type=jnp.float32) + bias_qkv
    head_shape = (row_count, H, DH)
    query_pre = qkv_full[:, :width].reshape(head_shape)
    key_pre = qkv_full[:, width : 2 * width].reshape(head_shape)
    value_pre = qkv_full[:, 2 * width :]
    query_out, query_normed, query_inv = norm_forward(query_pre, gain_query, 0.0)
    key_out, key_normed, key_inv = norm_forward(key_pre, gain_key, 0.0)
    image_shape = (image_count, own_len, width)
    query_low = query_out.astype(jnp.bfloat16).reshape(image_shape)
    key_low = key_out.astype(jnp.bfloat16).reshape(image_shape)
    value_low = value_pre.astype(jnp.bfloat16).reshape(image_shape)
    key_all, value_all = (
        lax.all_gather(key_low, "group", axis=1, tiled=True),
        lax.all_gather(value_low, "group", axis=1, tiled=True),
    )
    attn_out, log_sum = lax.map(
        partial(attend_block, masks=head_masks, scale_factor=scale_factor),
        (in_blocks(query_low), in_blocks(key_all), in_blocks(value_all)),
    )
    attn_low = unblock(attn_out).reshape(row_count, width).astype(jnp.bfloat16)
    resid_mid = resid_in + jnp.dot(attn_low, w_out, preferred_element_type=jnp.float32) + bias_out
    ln_two_out, normed_two, inv_two = norm_forward(resid_mid, gain_two, bias_two)
    act_two = ln_two_out.astype(jnp.bfloat16)
    hidden_pre = jnp.dot(act_two, w_fc1, preferred_element_type=jnp.float32) + bias_fc1
    hidden_low = jax.nn.gelu(hidden_pre, approximate=False).astype(jnp.bfloat16)
    result = resid_mid + jnp.dot(hidden_low, w_fc2, preferred_element_type=jnp.float32) + bias_fc2
    out_tokens = result.astype(jnp.bfloat16).reshape(tokens.shape)
    regathered = lax.all_gather(shard_low, "group", axis=0, tiled=True)
    back_qkv, back_out, back_fc1, back_fc2 = split_params(regathered)[:4]
    grad_res = cotangent.astype(jnp.float32).reshape(row_count, width)
    grad_mlp = cotangent.reshape(row_count, width)
    d_bias_fc2 = jnp.sum(grad_res, 0)
    d_w_fc2 = cross_dot(hidden_low, grad_mlp)
    grad_pre = (back_dot(grad_mlp, back_fc2) * gelu_slope(hidden_pre)).astype(jnp.bfloat16)
    d_bias_fc1 = jnp.sum(grad_pre.astype(jnp.float32), 0)
    d_w_fc1 = cross_dot(act_two, grad_pre)
    grad_norm_two = back_dot(grad_pre, back_fc1)
    d_gain_two = jnp.sum(grad_norm_two * normed_two, 0)
    d_bias_two = jnp.sum(grad_norm_two, 0)
    grad_mid = grad_res + norm_backward(grad_norm_two, normed_two, inv_two, gain_two)
    grad_proj = grad_mid.astype(jnp.bfloat16)
    d_bias_out = jnp.sum(grad_proj.astype(jnp.float32), 0)
    d_w_out = cross_dot(attn_low, grad_proj)
    grad_attn = back_dot(grad_proj, back_out).astype(jnp.bfloat16).reshape(image_shape)
    grad_q, grad_k_all, grad_v_all = lax.map(
        partial(local_back, masks=head_masks, scale_factor=scale_factor),
        (
            in_blocks(query_low),
            in_blocks(key_all),
            in_blocks(value_all),
            in_blocks(grad_attn),
            log_sum,
        ),
    )
    grad_key, grad_value = (
        lax.psum_scatter(
            unblock(grad_k_all).astype(jnp.bfloat16), "group", scatter_dimension=1, tiled=True
        ).astype(jnp.float32),
        lax.psum_scatter(
            unblock(grad_v_all).astype(jnp.bfloat16), "group", scatter_dimension=1, tiled=True
        ).astype(jnp.float32),
    )
    grad_query_n = unblock(grad_q).reshape(head_shape).astype(jnp.bfloat16).astype(jnp.float32)
    grad_key_n = grad_key.reshape(head_shape).astype(jnp.bfloat16).astype(jnp.float32)
    grad_value_n = grad_value.reshape(row_count, width).astype(jnp.bfloat16).astype(jnp.float32)
    d_gain_query = jnp.sum(grad_query_n * query_normed, (0, 1))
    d_gain_key = jnp.sum(grad_key_n * key_normed, (0, 1))
    grad_query_pre = norm_backward(grad_query_n, query_normed, query_inv, gain_query).reshape(
        row_count, width
    )
    grad_key_pre = norm_backward(grad_key_n, key_normed, key_inv, gain_key).reshape(
        row_count, width
    )
    grad_qkv = jnp.concatenate([grad_query_pre, grad_key_pre, grad_value_n], 1).astype(jnp.bfloat16)
    d_bias_qkv = jnp.sum(grad_qkv.astype(jnp.float32), 0)
    d_w_qkv = cross_dot(act_one, grad_qkv)
    grad_norm_one = back_dot(grad_qkv, back_qkv)
    d_gain_one = jnp.sum(grad_norm_one * normed_one, 0)
    d_bias_one = jnp.sum(grad_norm_one, 0)
    grad_in = grad_mid + norm_backward(grad_norm_one, normed_one, inv_one, gain_one)
    grad_tokens = grad_in.astype(jnp.bfloat16).reshape(tokens.shape)
    local_grad = jnp.concatenate(
        [
            member.reshape(-1)
            for member in (
                d_w_qkv,
                d_w_out,
                d_w_fc1,
                d_w_fc2,
                d_gain_one,
                d_bias_one,
                d_bias_qkv,
                d_gain_query,
                d_gain_key,
                d_bias_out,
                d_gain_two,
                d_bias_two,
                d_bias_fc1,
                d_bias_fc2,
            )
        ]
    )
    group_grad = lax.psum_scatter(
        local_grad.astype(jnp.bfloat16), "group", scatter_dimension=0, tiled=True
    ).astype(jnp.float32)
    grad_total = lax.psum(group_grad, "replica")
    momentum_new = MOMENT * momentum + grad_total
    weight_new = weight - rate[0] * (grad_total + MOMENT * momentum_new)
    step_value = step[0].astype(jnp.float32)
    ema_decay = jnp.minimum(DECAY_MAX, (1.0 + step_value) / (10.0 + step_value))
    average_new = ema_decay * average + (1.0 - ema_decay) * weight_new
    return (
        out_tokens,
        grad_tokens,
        grad_total,
        momentum_new,
        average_new,
        weight_new,
        weight_new.astype(jnp.bfloat16),
    )


def solution(mesh):
    in_specs = (
        P("replica", "group", None),
        P("replica", "group", None),
        P("group"),
        P("group"),
        P("group"),
        P(),
        P(),
    )
    out_specs = (
        P("replica", "group", None),
        P("replica", "group", None),
        P("group"),
        P("group"),
        P("group"),
        P("group"),
        P("group"),
    )
    return jax.shard_map(
        per_device, mesh=mesh, in_specs=in_specs, out_specs=out_specs, check_vma=False
    )
```

profile of v0, /device:TPU:0, one launch (start us, length us, event | category | flops | bytes accessed | tf_op | source)
XLA Modules:
  0.0 935.1 jit_solution(8608521233848531671)
XLA Ops:
  7.2 1.6 convert_element_type.177
  8.8 10.9 %reshape.335 = bf16[1,1,443648]{2,1,0:T(2,128)(2,1)} reshape(bf16[443648]{0:T(1024)(128)(2,1)S(1)} %convert_element_type.177) | data formatting | bytes 1774592
  21.7 51.8 %all-gather.9.cloned.1.call-done = bf16[4,1,443648]{2,1,0:T(2,128)(2,1)} async-done(((bf16[1,1,443648]{2,1,0:T(2,128)(2,1)}), bf16[4,1,443648]{2,1,0:T(2,128)(2,1)}) %all-gather.9.cloned.1.call-update) | async-done | bytes 3549200 | tf_op jit(solution)/shard_map/all_gather | solution.py:186
  73.5 78.3 %reduce.13 = bf16[4,443648]{1,0:T(4,128)(2,1)} reduce(bf16[4,1,443648]{2,1,0:T(2,128)(2,1)} %all-gather.9.cloned.1.call-done, bf16[]{:T(256)} %constant.199), dimensions={1}, to_apply=%all-gather.reduce_sub_computation | reduce | bytes 7098370 | tf_op jit(solution)/shard_map/all_gather | solution.py:186
  151.8 3.3 reshape.336
  159.8 2.9 reshape.314
  163.9 2.0 convolution_add_fusion
  168.6 2.4 copy.69
  172.9 2.5 mul.382
  176.4 1.6 sub.161
  178.0 3.3 multiply_convert_fusion.1
  182.8 3.2 fusion.70
  186.3 3.2 reshape.322
  189.5 2.2 reshape.321
  193.5 1.4 mul.374
  196.5 2.9 multiply_convert_fusion.2
  201.5 3.7 copy.71
  205.2 17.9 %all-gather.7.cloned.1.call-done = bf16[2,1024,384]{2,1,0:T(8,128)(2,1)} async-done(((bf16[2,256,384]{2,1,0:T(8,128)(2,1)}), bf16[2,1024,384]{2,1,0:T(8,128)(2,1)}) %all-gather.7.cloned.1.call-update) | async-done | bytes 1572880 | tf_op jit(solution)/shard_map/all_gather | solution.py:236
  223.1 15.4 %while.48 = (s32[]{:T(128)}, f32[2,256,384]{2,1,0:T(8,128)S(1)}, f32[6,2,256]{2,1,0:T(2,128)S(1)}, bf16[6,384]{1,0:T(8,128)(2,1)S(1)}, bf16[2,256,384]{2,1,0:T(8...) while((s32[]{:T(128)}, f32[2,256,384]{2,1,0:T(8,128)S(1)}, ...), condition=%wide.region_9.10_spmd.clone, body=%wide.region_6.9_spmd.clone.sunk | while | flops 811400704 | bytes 17714324 | solution.py:105
  240.0 8.8 fusion.34
  248.8 2.3 fusion.73
  251.1 1.7 multiply_reduce_fusion.2
  255.1 70.3 %while.49 = (s32[]{:T(128)}, f32[2,256,384]{2,1,0:T(8,128)}, f32[2,1024,384]{2,1,0:T(8,128)}, f32[2,1024,384]{2,1,0:T(8,128)}, bf16[6,384]{1,0:T(8,128)(2,1)S(1)...) while((s32[]{:T(128)}, f32[2,256,384]{2,1,0:T(8,128)}, ...), condition=%wide.region_16.17_spmd.clone, body=%wide.region_14.16_spmd.clone.sunk | while | flops 2023554560 | bytes 92814896 | solution.py:165
  255.3 2.1 fusion.125
  265.3 1.7 copy-done.4
  267.0 2.1 fusion.125
  277.0 1.7 copy-done.4
  278.7 2.1 fusion.125
  287.0 1.4 select_add_fusion.4
  288.6 1.7 copy-done.4
  290.4 2.1 fusion.125
  298.7 1.4 select_add_fusion.4
  300.3 1.7 copy-done.4
  302.1 2.1 fusion.125
  312.0 1.7 copy-done.4
  313.7 2.1 fusion.125
  323.7 1.7 copy-done.4
  325.4 2.1 convert_element_type.230
  327.5 61.8 %copy.90 = bf16[2,1024,384]{0,2,1:T(8,128)(2,1)} copy(bf16[2,1024,384]{2,1,0:T(8,128)(2,1)S(1)} %convert_element_type.230) | data formatting | bytes 3145728
  389.2 162.7 %reshape.337 = bf16[1024,768]{1,0:T(8,128)(2,1)} reshape(bf16[1024,384,2]{2,1,0:T(8,128)(2,1)} %bitcast.29) | data formatting | bytes 3145728
  557.2 2.4 copy.80
  559.7 1.6 copy.74
  565.1 2.5 convolution_convert_fusion
  567.6 1.6 reshape.330
  570.6 3.5 convolution_convert_fusion.1
  574.1 3.7 reshape.329
  577.8 3.1 multiply_reduce_fusion.4
  586.1 56.0 %reshape.338 = bf16[256,384,2]{2,1,0:T(8,128)(2,1)} reshape(bf16[256,768]{1,0:T(8,128)(2,1)} %reduce-scatter.7.cloned.1.call-done) | data formatting | bytes 786432
  642.1 23.3 %copy.91 = bf16[2,256,384]{1,0,2:T(2,128)(2,1)S(1)} copy(bf16[2,256,384]{0,2,1:T(8,128)(2,1)} %bitcast.123) | data formatting | bytes 786432
  667.9 3.1 multiply_reduce_fusion.3
  674.7 2.3 copy.83
  678.0 2.3 copy.86
  680.4 4.6 fusion.57
  685.0 1.4 fusion.67
  686.5 4.0 multiply_reduce_fusion.5
  690.5 1.6 convolution_convert_fusion.2
  692.1 2.8 reshape.327
  694.9 50.5 %concatenate.9 = bf16[1774592]{0:T(1024)(128)(2,1)} concatenate(bf16[442368]{0:T(1024)(128)(2,1)} %reshape.327, bf16[147456]{0:T(1024)(128)(2,1)} %reshape.328, bf16[589824]{0:T(1024)(128)(2,1)S(1)} %copy-done.38, bf16[589824]{0:T(1024)(128)(2,1)S(1)} %copy-done.37, bf16[384]{0:T(512)(128)(2,1)} %get-tuple-element.265, bf16[384]{0:T(512)(128)(2,1)} %get-tuple-element.274, ...), dimensions={0} | concatenate | bytes 7098368 | tf_op jit(solution)/shard_map/concatenate | solution.py:304
  747.3 73.6 %all-reduce.6.cloned.1.call-done = bf16[1774592]{0:T(1024)(128)(2,1)} async-done(((bf16[1774592]{0:T(1024)(128)(2,1)}), bf16[1774592]{0:T(1024)(128)(2,1)}) %all-reduce.6.cloned.1.call-update) | async-done | bytes 3549200
  820.9 2.9 dynamic-slice_convert_fusion
  825.2 3.2 fusion.49
  829.6 90.3 %all-reduce.4.cloned.1.call-done = f32[443648]{0:T(1024)} async-done(((f32[443648]{0:T(1024)}), f32[443648]{0:T(1024)}) %all-reduce.4.cloned.1.call-update) | async-done | bytes 1774608 | tf_op jit(solution)/shard_map/psum | solution.py:328
  919.8 4.0 fusion.69
  923.9 1.5 multiply_add_fusion
  (404 shorter events, 111.0 us)
Async XLA Ops:
  7.2 66.3 %all-gather.9.cloned.1.call-start = ((), (), s32[]{:S(2)}) async-start(), calls=%async_computation.6 | async-start | bytes 8872960 | tf_op jit(solution)/shard_map/all_gather | solution.py:186
  8.8 11.0 %copy-start.15 = (bf16[2,256,384]{2,1,0:T(8,128)(2,1)S(1)}, bf16[2,256,384]{2,1,0:T(8,128)(2,1)}, u32[]{:S(2)}) copy-start(bf16[2,256,384]{2,1,0:T(8,128)(2,1)} %param.11) | copy-start | bytes 1179652
  19.7 181.8 %all-gather.5.cloned.1.call-start = ((), (), s32[]{:S(2)}) async-start(), calls=%async_computation.2 | async-start | bytes 1966080 | tf_op jit(solution)/shard_map/all_gather | solution.py:235
  155.1 8.7 copy-start.8
  159.8 18.2 %copy-start.60 = (f32[384]{0:T(512)}, f32[384]{0:T(512)S(1)}, u32[]{:S(2)}) copy-start(f32[384]{0:T(512)S(1)} %mul.385) | copy-start | bytes 4612
  165.9 16.0 %copy-start.6 = (f32[512,1152]{1,0:T(8,128)}, f32[512,1152]{1,0:T(8,128)S(1)}, u32[]{:S(2)}) copy-start(f32[512,1152]{1,0:T(8,128)S(1)} %convolution_add_fusion) | copy-start | bytes 7077892
  168.6 6.8 copy-start.9
  171.1 6.9 copy-start.54
  178.0 8.0 copy-start.32
  181.4 41.8 %all-gather.7.cloned.1.call-start = ((), (), s32[]{:S(2)}) async-start(), calls=%async_computation.3 | async-start | bytes 1966080 | tf_op jit(solution)/shard_map/all_gather | solution.py:236
  182.7 3.3 copy-start.74
  182.7 3.4 slice-start
  182.7 403.4 %reduce-scatter.7.cloned.1.call-start = ((), (), s32[]{:S(2)}) async-start(), calls=%async_computation.7 | async-start | bytes 1966080
  186.0 3.5 copy-start.39
  186.1 9.4 %copy-start.62 = (f32[384]{0:T(512)}, f32[384]{0:T(512)S(1)}, u32[]{:S(2)}) copy-start(f32[384]{0:T(512)S(1)} %mul.377) | copy-start | bytes 4612
  186.3 5.4 copy-start.29
  191.9 3.0 copy-start.11
  192.6 3.0 copy-start.33
  193.5 5.9 copy-start.26
  195.0 5.7 copy-start.27
  199.4 23.8 %copy-start.51 = (f32[2,256,384]{2,1,0:T(8,128)S(1)}, f32[2,256,384]{2,1,0:T(8,128)}, u32[]{:S(2)}) copy-start(f32[2,256,384]{2,1,0:T(8,128)} %custom-call) | copy-start | bytes 2359300
  223.1 15.6 %copy-start.16 = (bf16[2,256,384]{2,1,0:T(8,128)(2,1)S(1)}, bf16[2,256,384]{2,1,0:T(8,128)(2,1)}, u32[]{:S(2)}) copy-start(bf16[2,256,384]{2,1,0:T(8,128)(2,1)} %param.11) | copy-start | bytes 1179652
  223.1 15.6 %copy-start.67 = (f32[384]{0:T(512)S(1)}, f32[384]{0:T(512)}, u32[]{:S(2)}) copy-start(f32[384]{0:T(512)} %get-tuple-element.321) | copy-start | bytes 4612
  239.4 13.4 %copy-start.21 = (f32[512,384]{1,0:T(8,128)}, f32[512,384]{1,0:T(8,128)S(1)}, u32[]{:S(2)}) copy-start(f32[512,384]{1,0:T(8,128)S(1)} %get-tuple-element.338) | copy-start | bytes 2359300
  240.0 8.8 copy-start.45
  240.0 8.8 copy-start.46
  389.2 163.4 %copy-start.68 = (f32[1,2,2,128]{3,2,1,0:T(2,128)S(1)}, f32[1,2,2,128]{3,2,1,0:T(2,128)}, u32[]{:S(2)}) copy-start(f32[1,2,2,128]{3,2,1,0:T(2,128)} %get-tuple-element.335) | copy-start | bytes 6148
  389.2 164.0 %copy-start.69 = (f32[1,2,2,128]{3,2,1,0:T(2,128)S(1)}, f32[1,2,2,128]{3,2,1,0:T(2,128)}, u32[]{:S(2)}) copy-start(f32[1,2,2,128]{3,2,1,0:T(2,128)} %get-tuple-element.333) | copy-start | bytes 6148
  551.9 3.0 copy-start.24
  551.9 4.1 copy-start.28
  552.0 133.1 %reduce-scatter.5.cloned.1.call-start = ((), (), s32[]{:S(2)}) async-start(), calls=%async_computation.4 | async-start | bytes 1966080 | tf_op jit(solution)/shard_map/reduce_scatter | solution.py:281
  557.2 6.5 copy-start.2
  565.1 255.8 %all-reduce.6.cloned.1.call-start = ((), (), s32[]{:S(2)}) async-start(), calls=%async_computation.8 | async-start | bytes 7098368
  567.6 2.9 copy-start.22
  570.6 7.2 copy-start.34
  570.6 7.2 copy-start.35
  574.1 8.1 copy-start.12
  574.1 8.1 copy-start.57
  665.4 6.9 copy-start.10
  665.4 6.9 copy-start.55
  673.7 6.6 copy-start.7
  673.8 6.6 copy-start.61
  673.8 6.6 copy-start.63
  680.4 6.1 copy-start.17
  680.4 6.1 copy-start.65
  680.4 6.1 copy-start.66
  686.5 4.0 copy-start.43
  686.5 4.0 copy-start.44
  686.5 4.0 copy-start.53
  690.5 4.4 copy-start.37
  690.5 4.4 copy-start.38
  690.5 4.4 copy-start.75
  690.5 4.4 copy-start.76
  745.4 79.7 %copy-start.23 = (f32[512,384]{1,0:T(8,128)S(1)}, f32[512,384]{1,0:T(8,128)}, u32[]{:S(2)}) copy-start(f32[512,384]{1,0:T(8,128)} %copy-done.21) | copy-start | bytes 2359300
  745.4 79.7 %copy-start.47 = (bf16[1536,384]{1,0:T(8,128)(2,1)S(1)}, bf16[1536,384]{1,0:T(8,128)(2,1)}, u32[]{:S(2)}) copy-start(bf16[1536,384]{1,0:T(8,128)(2,1)} %reshape.322) | copy-start | bytes 3538948
  745.5 79.7 %copy-start.77 = (f32[384]{0:T(512)S(1)}, f32[384]{0:T(512)}, u32[]{:S(2)}) copy-start(f32[384]{0:T(512)} %get-tuple-element.318) | copy-start | bytes 4612
  745.5 174.4 %all-reduce.4.cloned.1.call-start = ((), (), s32[]{:S(2)}) async-start(), calls=%async_computation.5 | async-start | bytes 3555328 | tf_op jit(solution)/shard_map/psum | solution.py:328
  825.1 3.3 copy-start.80
  825.1 3.3 copy-start.79
  825.1 3.3 copy-start.52
  825.2 3.3 copy-start.71
  825.2 3.3 copy-start.72
  828.4 91.5 %copy-start.20 = (f32[443648]{0:T(1024)S(1)}, f32[443648]{0:T(1024)}, u32[]{:S(2)}) copy-start(f32[443648]{0:T(1024)} %param.13) | copy-start | bytes 5323780
  919.8 4.0 copy-start.42
  (62 other events, 99.2 us)
Sparse Core Ops, SparseCore 0:
  19.8 53.6 all-gather.8
  181.5 19.8 all-gather.4
  203.5 19.6 all-gather.6
  552.1 28.0 reduce-scatter.6
  583.1 28.0 reduce-scatter.4
  745.6 75.2 all-reduce.5
  825.1 94.7 all-reduce.3
where the time goes:
time: 944 us; the launch traced here: 935 us
  local copies, waits for them, and re-layouts  471 us (50%)
  waiting for transfers between devices  234 us (25%)
  other arithmetic  128 us (14%)
  matrix products  83.4 us (9%)
  between operations  17.3 us (2%)
    unnamed x164, local copies, waits for them, and re-layouts  332 us
    psum x1, waiting for transfers between devices, per_device(): grad_total = lax.psum(group_grad, 'replica')  90.3 us
    all_gather x1, other arithmetic, per_device(): gathered = lax.all_gather(shard_low, 'group', axis=0, tiled=True)  78.3 us
    unnamed x9, waiting for transfers between devices  73.7 us
    all_gather x1, waiting for transfers between devices, per_device(): gathered = lax.all_gather(shard_low, 'group', axis=0, tiled=True)  51.8 us
    concatenate x1, local copies, waits for them, and re-layouts, per_device(): jnp.concatenate([member.reshape(-1) for member in (d_w_qkv, d_w_out, d_w_...  50.5 us
    while x84, local copies, waits for them, and re-layouts  27.4 us
  transfers between devices with their start and end apart: 7, of which 4 were waited for; matrix products, arithmetic and copies ran while one was open for 17% of the time, Pallas kernels for 0%

commit v1 on v0

v1 whole, which is shorter than its diff:
```python
import jax
import jax.numpy as jnp
from jax import lax
from jax.experimental import pallas as pl
from jax.experimental.pallas import tpu as pltpu
from jax.sharding import PartitionSpec as P

D = 384
H = 6
DH = 64
FF = 1536
EPSILON = 1e-06
MOMENT = 0.9
DECAY_MAX = 0.999
INV_ROOT_TWO = 0.7071067811865476
INV_ROOT_TAU = 0.3989422804014327
SCALE = DH ** (-0.5)

ROW_OUT = 3456
ROW_FC1 = 4608
ROW_FC2 = 9216
ROW_VEC = 13824
ROWS = 13864
QUARTER = 3466
PAD_Q = 3488
ROWS_A = ROW_VEC - ROW_OUT
PAD_A = 10496
PAD_B = 3584

F32 = jnp.float32
BF16 = jnp.bfloat16


def dot_nn(a, b):
    return lax.dot_general(a, b, (((1,), (0,)), ((), ())), preferred_element_type=F32)


def dot_nt(a, b):
    return lax.dot_general(a, b, (((1,), (1,)), ((), ())), preferred_element_type=F32)


def dot_tn(a, b):
    return lax.dot_general(a, b, (((0,), (0,)), ((), ())), preferred_element_type=F32)


def row_of(vec, start, count):
    return jnp.concatenate([vec[start + i : start + i + 1] for i in range(count)], axis=1)


def norm(values):
    center = values - jnp.mean(values, -1, keepdims=True)
    inv = lax.rsqrt(jnp.mean(center * center, -1, keepdims=True) + EPSILON)
    return center * inv, inv


def norm_back(grad_norm, normed, inv):
    inner = jnp.mean(grad_norm * normed, -1, keepdims=True)
    return inv * (grad_norm - jnp.mean(grad_norm, -1, keepdims=True) - normed * inner)


def head_mean_matrix():
    r = lax.broadcasted_iota(jnp.int32, (256, 128), 0)
    c = lax.broadcasted_iota(jnp.int32, (256, 128), 1)
    return jnp.where((r % 128) // DH == c // DH, 1.0 / DH, 0.0).astype(BF16)


def head_mean(x, matrix):
    hi = x.astype(BF16)
    lo = (x - hi.astype(F32)).astype(BF16)
    return dot_nn(jnp.concatenate([hi, lo], axis=1), matrix)


def lane_head(rows, h):
    lane = lax.broadcasted_iota(jnp.int32, (rows, 128), 1)
    return (lane // DH) == h, lane - DH * (1 - h)


def qkv_attend_kernel(
    xo_ref, xt_ref, wf_ref, vec_ref,
    act_ref, w2_ref, qx_ref, k_ref, v_ref, out_ref, nq_ref, iq_ref, nk_ref, ik_ref,
    flat, q_s,
):
    rows = xo_ref.shape[0]
    vec = vec_ref[...].astype(F32)
    gain_one, bias_one, bias_qkv = row_of(vec, 0, 3), row_of(vec, 3, 3), row_of(vec, 6, 9)
    gains = vec[15:16]
    gain_q = jnp.concatenate([gains[:, :DH], gains[:, :DH]], axis=1)
    gain_k = jnp.concatenate([gains[:, DH:], gains[:, DH:]], axis=1)
    flat[...] = wf_ref[...].astype(F32)
    for j in range(9):
        w2_ref[:, 128 * j : 128 * j + 128] = flat[pl.ds(j, D, stride=9), :].astype(BF16)
    step = 256

    def ln(ref, base):
        def body(i, c):
            at = pl.multiple_of(i * step, step)
            n, _ = norm(ref[pl.ds(at, step), :].astype(F32))
            act_ref[pl.ds(at + base, step), :] = (n * gain_one + bias_one).astype(BF16)
            return c
        lax.fori_loop(0, rows // step, body, 0)

    ln(xo_ref, 0)
    ln(xt_ref, rows)
    matrix = head_mean_matrix()

    def heads(x, gain, n_ref, i_ref, at, p):
        c = x - head_mean(x, matrix)
        inv = lax.rsqrt(head_mean(c * c, matrix) + EPSILON)
        n = c * inv
        n_ref[pl.ds(at, step), 128 * p : 128 * p + 128] = n
        i_ref[pl.ds(at, step), 128 * p : 128 * p + 128] = inv
        return n * gain

    def project_q(i, c):
        at = pl.multiple_of(i * step, step)
        x = dot_nn(act_ref[pl.ds(at, step), :], w2_ref[:, :D]) + bias_qkv[:, :D]
        for p in range(3):
            y = heads(x[:, 128 * p : 128 * p + 128], gain_q, nq_ref, iq_ref, at, p)
            q_s[p, pl.ds(at, step), :] = y.astype(BF16) * BF16(SCALE)
        return c

    lax.fori_loop(0, rows // step, project_q, 0)

    def project_kv(i, c):
        at = pl.multiple_of(i * step, step)
        x = dot_nn(act_ref[pl.ds(at, step), :], w2_ref[:, D:]) + bias_qkv[:, D:]
        for p in range(3):
            y = heads(x[:, 128 * p : 128 * p + 128], gain_k, nk_ref, ik_ref, at, p)
            k_ref[p, pl.ds(at, step), :] = y.astype(BF16)
            v_ref[p, pl.ds(at, step), :] = x[:, D + 128 * p : D + 128 * p + 128].astype(BF16)
        return c

    lax.fori_loop(0, 2 * rows // step, project_kv, 0)

    def attend(p, c):
        q, k, v = q_s[p], k_ref[p], v_ref[p]
        parts = []
        for h in range(2):
            mine, _ = lane_head(2 * rows, h)
            own, other = lane_head(rows, h)
            qm = jnp.where(own, q, BF16(0.0))
            e = jnp.exp(dot_nt(qm, k)).astype(BF16)
            o = dot_nn(e, jnp.where(mine, v, BF16(1.0)))
            total = pltpu.roll(o, DH, 1)
            parts.append(o / total)
            neg = -jnp.log(o)
            hi = neg.astype(BF16)
            mid_f = neg - hi.astype(F32)
            mid = mid_f.astype(BF16)
            low = (mid_f - mid.astype(F32)).astype(BF16)
            spare = jnp.where(other == 0, hi, jnp.where(other == 1, mid, jnp.where(other == 2, low, BF16(0.0))))
            qx_ref[2 * p + h] = jnp.where(own, qm, spare)
        own, _ = lane_head(rows, 0)
        out_ref[p] = jnp.where(own, parts[0], parts[1])
        return c

    lax.fori_loop(0, 3, attend, 0)


def mlp_kernel(
    x_ref, o_ref, cot_ref, q0_ref, q1_ref, q2_ref, q3_ref,
    out_ref, gmid_ref, gattn_ref, da_ref, dv_ref,
    flat, wo_s, w1_s, w2_s, act_s, n_s, mid_s, gn_s, y_s, db1_s,
):
    rows = x_ref.shape[0]
    flat[0:10, :] = q0_ref[ROW_OUT : ROW_OUT + 10, :].astype(F32)
    flat[10 : 10 + QUARTER, :] = q1_ref[0:QUARTER, :].astype(F32)
    flat[10 + QUARTER : 10 + 2 * QUARTER, :] = q2_ref[0:QUARTER, :].astype(F32)
    flat[10 + 2 * QUARTER : 10 + 3 * QUARTER, :] = q3_ref[0:QUARTER, :].astype(F32)
    vec = flat[ROWS_A : ROWS_A + 40, :]
    bias_out, gain_two, bias_two = row_of(vec, 16, 3), row_of(vec, 19, 3), row_of(vec, 22, 3)
    bias_fc1, bias_fc2 = row_of(vec, 25, 12), row_of(vec, 37, 3)
    for j in range(3):
        wo_s[:, 128 * j : 128 * j + 128] = flat[pl.ds(j, D, stride=3), :].astype(BF16)
        w2_s[:, 128 * j : 128 * j + 128] = flat[pl.ds(ROW_FC2 - ROW_OUT + j, FF, stride=3), :].astype(BF16)
    for j in range(12):
        w1_s[:, 128 * j : 128 * j + 128] = flat[pl.ds(ROW_FC1 - ROW_OUT + j, D, stride=12), :].astype(BF16)

    attn = jnp.concatenate([o_ref[p].astype(BF16) for p in range(3)], axis=1)
    mid = x_ref[...].astype(F32) + dot_nn(attn, wo_s[...]) + bias_out
    mid_s[...] = mid
    n, inv = norm(mid)
    n_s[...] = n
    act_s[...] = (n * gain_two + bias_two).astype(BF16)
    y_s[...] = mid + bias_fc2
    gn_s[...] = jnp.zeros_like(gn_s)
    width = 256
    for f in range(FF // width):
        at = f * width
        w1 = w1_s[:, at : at + width]
        w2 = w2_s[at : at + width, :]
        x = dot_nn(act_s[...], w1) + bias_fc1[:, at : at + width]
        phi = 0.5 * (1.0 + lax.erf(x * INV_ROOT_TWO))
        hid = (x * phi).astype(BF16)
        slope = phi + x * jnp.exp(-0.5 * x * x) * INV_ROOT_TAU
        g = dot_nt(cot_ref[...], w2) * slope
        gb = g.astype(BF16)
        y_s[...] += dot_nn(hid, w2)
        gn_s[...] += dot_nt(gb, w1)
        dw2 = dot_tn(hid, cot_ref[...])
        for j in range(3):
            flat[pl.ds(ROW_FC2 - ROW_OUT + 3 * at + j, width, stride=3), :] = dw2[:, 128 * j : 128 * j + 128]
        dw1 = dot_tn(act_s[...], gb)
        for j in range(width // 128):
            flat[pl.ds(ROW_FC1 - ROW_OUT + at // 128 + j, D, stride=12), :] = dw1[:, 128 * j : 128 * j + 128]
        db1_s[:, at : at + width] = jnp.sum(gb.astype(F32), 0, keepdims=True)
    out_ref[...] = y_s[...].astype(BF16)
    gn = gn_s[...]
    cot = cot_ref[...].astype(F32)
    gmid = cot + norm_back(gn * gain_two, n_s[...], inv)
    gmid_ref[...] = gmid
    gproj = gmid.astype(BF16)
    gattn_ref[...] = dot_nt(gproj, wo_s[...]).astype(BF16)
    dwo = dot_tn(attn, gproj)
    for j in range(3):
        flat[pl.ds(j, D, stride=3), :] = dwo[:, 128 * j : 128 * j + 128]
    da_ref[0:ROWS_A, :] = flat[0:ROWS_A, :].astype(BF16)
    da_ref[ROWS_A:, :] = jnp.zeros((PAD_A - ROWS_A, 128), BF16)

    def put(at, row):
        for i in range(row.shape[1] // 128):
            dv_ref[at + i : at + i + 1, :] = row[:, 128 * i : 128 * i + 128]

    put(0, jnp.sum(gproj.astype(F32), 0, keepdims=True))
    put(3, jnp.sum(gn * n_s[...], 0, keepdims=True))
    put(6, jnp.sum(gn, 0, keepdims=True))
    put(9, db1_s[...])
    put(21, jnp.sum(cot, 0, keepdims=True))


def attend_back_kernel(
    xo_ref, xt_ref, act_ref, w2_ref, qx_ref, k_ref, v_ref, out_ref, nq_ref, iq_ref, nk_ref, ik_ref,
    vec_ref, ga_ref, gmid_ref, dv_ref,
    db_ref, go_ref, gt_ref,
    flat, ga_s, gq_s, gk_s, gv_s, gqkv_s, vrow_s,
):
    rows = xo_ref.shape[0]
    vec = vec_ref[...].astype(F32)
    gain_one = row_of(vec, 0, 3)
    gains = vec[15:16]
    gain_q = jnp.concatenate([gains[:, :DH], gains[:, :DH]], axis=1)
    gain_k = jnp.concatenate([gains[:, DH:], gains[:, DH:]], axis=1)
    matrix = head_mean_matrix()
    for p in range(3):
        ga_s[p] = ga_ref[:, 128 * p : 128 * p + 128]

    def back(p, c):
        k, v, ga = k_ref[p], v_ref[p], ga_s[p]
        inner = -float(DH) * head_mean(ga.astype(F32) * out_ref[p], matrix)
        inner = pltpu.roll(inner, DH, 1)
        hi = inner.astype(BF16)
        mid_f = inner - hi.astype(F32)
        mid = mid_f.astype(BF16)
        low = (mid_f - mid.astype(F32)).astype(BF16)
        gq_t = jnp.zeros((128, rows), F32)
        gk = jnp.zeros((2 * rows, 128), F32)
        gv = jnp.zeros((2 * rows, 128), F32)
        for h in range(2):
            mine, other_all = lane_head(2 * rows, h)
            own, other = lane_head(rows, h)
            ones = jnp.where((other_all >= 0) & (other_all <= 2), 1.0, 0.0).astype(BF16)
            qx = qx_ref[2 * p + h]
            spare = jnp.where(other == 0, hi, jnp.where(other == 1, mid, jnp.where(other == 2, low, BF16(0.0))))
            gax = jnp.where(own, ga, spare)
            prob = jnp.exp(dot_nt(jnp.where(mine, k, ones), qx))
            gprob = dot_nt(jnp.where(mine, v, ones), gax)
            gs = (prob * gprob).astype(BF16)
            gv = gv + dot_nn(prob.astype(BF16), jnp.where(own, ga, BF16(0.0)))
            gk = gk + dot_nn(gs, jnp.where(own, qx, BF16(0.0)))
            gq_t = gq_t + dot_tn(jnp.where(mine, k, BF16(0.0)), gs)
        gq_s[p] = (gq_t.T * SCALE).astype(BF16).astype(F32)
        gk_s[p] = gk.astype(BF16).astype(F32)
        gv_s[p] = gv.astype(BF16)
        return c

    lax.fori_loop(0, 3, back, 0)

    def head_back(u, n, inv, gain):
        dn = u * gain
        return inv * (dn - head_mean(dn, matrix) - n * head_mean(dn * n, matrix))

    def put(at, row):
        for i in range(row.shape[1] // 128):
            vrow_s[at + i : at + i + 1, :] = row[:, 128 * i : 128 * i + 128]

    dgq = jnp.zeros((1, 128), F32)
    dgk = jnp.zeros((1, 128), F32)
    for p in range(3):
        sl = slice(128 * p, 128 * p + 128)
        n = nq_ref[:, sl]
        u = gq_s[p]
        dgq = dgq + jnp.sum(u * n, 0, keepdims=True)
        gqkv_s[0:rows, sl] = head_back(u, n, iq_ref[:, sl], gain_q).astype(BF16)
        n = nk_ref[:, sl]
        u = gk_s[p]
        dgk = dgk + jnp.sum(u * n, 0, keepdims=True)
        gqkv_s[:, D + 128 * p : D + 128 * p + 128] = head_back(u, n, ik_ref[:, sl], gain_k).astype(BF16)
        gqkv_s[:, 2 * D + 128 * p : 2 * D + 128 * p + 128] = gv_s[p]
    dgq = dgq + pltpu.roll(dgq, DH, 1)
    dgk = dgk + pltpu.roll(dgk, DH, 1)
    own, _ = lane_head(1, 0)
    put(15, jnp.where(own, dgq, dgk))
    gqkv_q = gqkv_s[0:rows, 0:D]
    gqkv_kv = gqkv_s[:, D:]
    put(6, jnp.sum(gqkv_q.astype(F32), 0, keepdims=True))
    put(9, jnp.sum(gqkv_kv.astype(F32), 0, keepdims=True))
    dwq = dot_tn(act_ref[0:rows, :], gqkv_q)
    dwkv = dot_tn(act_ref[...], gqkv_kv)
    for j in range(3):
        flat[pl.ds(j, D, stride=9), :] = dwq[:, 128 * j : 128 * j + 128]
    for j in range(6):
        flat[pl.ds(3 + j, D, stride=9), :] = dwkv[:, 128 * j : 128 * j + 128]
    db_ref[0:ROW_OUT, :] = flat[...].astype(BF16)
    u_own = dot_nt(gqkv_q, w2_ref[:, 0:D]) + dot_nt(gqkv_kv[0:rows], w2_ref[:, D:])
    u_oth = dot_nt(gqkv_kv[rows:], w2_ref[:, D:])
    n_own, inv_own = norm(xo_ref[...].astype(F32))
    n_oth, inv_oth = norm(xt_ref[...].astype(F32))
    put(0, jnp.sum(u_own * n_own, 0, keepdims=True) + jnp.sum(u_oth * n_oth, 0, keepdims=True))
    put(3, jnp.sum(u_own, 0, keepdims=True) + jnp.sum(u_oth, 0, keepdims=True))
    go_ref[...] = gmid_ref[...] + norm_back(u_own * gain_one, n_own, inv_own)
    gt_ref[...] = norm_back(u_oth * gain_one, n_oth, inv_oth).astype(BF16)
    vrow_s[16:40, :] = dv_ref[...]
    vrow_s[40:128, :] = jnp.zeros((88, 128), F32)
    db_ref[ROW_OUT:, :] = vrow_s[...].astype(BF16)


def shape(*dims, dtype=BF16):
    return jax.ShapeDtypeStruct(dims, dtype)


def vmem(*dims, dtype=BF16):
    return pltpu.VMEM(dims, dtype)


def per_device(tokens, cotangent, weight, momentum, average, rate, step, replicas):
    _, own_len, width = tokens.shape
    rows = 2 * own_len
    place = lax.axis_index("group")
    x, c = place // 2, place % 2
    rep = lax.axis_index("replica")

    def swap(a, bit):
        return lax.ppermute(a, "group", [(i, i ^ bit) for i in range(4)])

    def swap_rep(a, bit):
        return lax.ppermute(a, "replica", [(i, i ^ bit) for i in range(replicas)])

    def pick(a, i):
        return lax.dynamic_index_in_dim(a, i, 0, keepdims=False)

    def across(a):
        return jnp.concatenate([pick(a, x), swap(pick(a, 1 - x), 2)], axis=0)

    xo = across(tokens)
    xt = swap(xo, 1)
    shard = jnp.pad(weight.reshape(QUARTER, 128).astype(BF16), ((0, PAD_Q - QUARTER), (0, 0)))
    beside = swap(shard, 1)
    half = PAD_Q // 2

    def half_of(a):
        return lax.dynamic_slice_in_dim(a, c * half, half, 0)

    def both(mine):
        theirs = swap(mine, 1)
        return jnp.where(c == 0, jnp.concatenate([mine, theirs]), jnp.concatenate([theirs, mine]))

    first = both(swap(half_of(jnp.where(c == x, shard, beside)), 2))
    second = both(swap(half_of(jnp.where(c == x, beside, shard)), 2))
    even = jnp.where(c == 0, shard, beside)
    odd = jnp.where(c == 0, beside, shard)
    q0 = jnp.where(x == 0, even, first)
    q1 = jnp.where(x == 0, odd, second)
    q2 = jnp.where(x == 0, second, even)
    q3 = jnp.where(x == 0, first, odd)
    vec = q3[QUARTER - 40 : QUARTER]

    act, w2, qx, k, v, out, nq, iq, nk, ik = pl.pallas_call(
        qkv_attend_kernel,
        out_shape=(
            shape(2 * rows, D), shape(D, 3 * D), shape(H, rows, 128),
            shape(3, 2 * rows, 128), shape(3, 2 * rows, 128), shape(3, rows, 128, dtype=F32),
            shape(rows, D, dtype=F32), shape(rows, D, dtype=F32),
            shape(2 * rows, D, dtype=F32), shape(2 * rows, D, dtype=F32),
        ),
        scratch_shapes=[vmem(ROW_OUT, 128, dtype=F32), vmem(3, rows, 128)],
        name="qkv_attend",
    )(xo, xt, q0[:ROW_OUT], vec)
    cot = across(cotangent)
    y, gmid, gattn, da, dv = pl.pallas_call(
        mlp_kernel,
        out_shape=(
            shape(rows, D), shape(rows, D, dtype=F32), shape(rows, D),
            shape(PAD_A, 128), shape(24, 128, dtype=F32),
        ),
        scratch_shapes=[
            vmem(ROWS_A + 40, 128, dtype=F32), vmem(D, D), vmem(D, FF), vmem(FF, D), vmem(rows, D),
            vmem(rows, D, dtype=F32), vmem(rows, D, dtype=F32), vmem(rows, D, dtype=F32),
            vmem(rows, D, dtype=F32), vmem(1, FF, dtype=F32),
        ],
        name="mlp",
    )(xo, out, cot, q0, q1, q2, q3)
    db, go, gt = pl.pallas_call(
        attend_back_kernel,
        out_shape=(shape(PAD_B, 128), shape(rows, D, dtype=F32), shape(rows, D)),
        scratch_shapes=[
            vmem(ROW_OUT, 128, dtype=F32), vmem(3, rows, 128), vmem(3, rows, 128, dtype=F32),
            vmem(3, 2 * rows, 128, dtype=F32), vmem(3, 2 * rows, 128), vmem(2 * rows, 3 * D),
            vmem(128, 128, dtype=F32),
        ],
        name="attend_back",
    )(xo, xt, act, w2, qx, k, v, out, nq, iq, nk, ik, vec, gattn, gmid, dv)

    def give_back(mine):
        kept, sent = mine[:own_len], mine[own_len:]
        got = swap(sent, 2)
        return jnp.where(x == 0, jnp.stack([kept, got]), jnp.stack([got, kept]))

    out_tokens = give_back(y)
    grad_tokens = give_back((go + swap(gt, 1).astype(F32)).astype(BF16))

    bits = []
    b = 1
    while b < replicas:
        bits.append(b)
        b *= 2
    moves = [(swap, 1, c), (swap, 2, x)] + [(swap_rep, b, (rep // b) % 2) for b in bits]

    def reduce_all(part):
        for move, bit, side in moves[:-1]:
            n = part.shape[0] // 2
            sent = lax.dynamic_slice_in_dim(part, (1 - side) * n, n, 0)
            kept = lax.dynamic_slice_in_dim(part, side * n, n, 0)
            part = (kept.astype(F32) + move(sent, bit).astype(F32)).astype(BF16)
        move, bit, side = moves[-1]
        part = (part.astype(F32) + move(part, bit).astype(F32)).astype(BF16)
        for move, bit, side in moves[:-1][::-1]:
            got = move(part, bit)
            part = jnp.where(side == 0, jnp.concatenate([part, got]), jnp.concatenate([got, part]))
        return part

    sum_a = reduce_all(da)
    sum_b = reduce_all(db)
    full = jnp.concatenate([sum_b[:ROW_OUT], sum_a[:ROWS_A], sum_b[ROW_OUT : ROW_OUT + 40]]).astype(F32)
    grad = lax.dynamic_slice_in_dim(full, place * QUARTER, QUARTER, 0).reshape(-1)
    momentum_new = MOMENT * momentum + grad
    weight_new = weight - rate[0] * (grad + MOMENT * momentum_new)
    step_value = step[0].astype(F32)
    decay = jnp.minimum(DECAY_MAX, (1.0 + step_value) / (10.0 + step_value))
    average_new = decay * average + (1.0 - decay) * weight_new
    return (
        out_tokens, grad_tokens, grad, momentum_new, average_new, weight_new, weight_new.astype(BF16),
    )


def solution(mesh):
    tok, flat = P("replica", "group", None), P("group")

    def body(*args):
        return per_device(*args, replicas=mesh.shape["replica"])

    return jax.shard_map(
        body,
        mesh=mesh,
        in_specs=(tok, tok, flat, flat, flat, P(), P()),
        out_specs=(tok, tok, flat, flat, flat, flat, flat),
        check_vma=False,
    )
```

time: 944 us -> 204 us (0.22)
  local copies, waits for them, and re-layouts: 471 us -> 8.55 us
  waiting for transfers between devices: 234 us -> 80 us
  other arithmetic: 128 us -> 35.4 us
  matrix products: 83.4 us -> 0 us
  Pallas kernels: 0 us -> 43.9 us
  starting transfers between devices: 0.95 us -> 32.2 us
  between operations: 17.3 us -> 2.37 us
    unnamed x164 -> x26, local copies, waits for them, and re-layouts: 332 us -> 0.94 us
    psum x1 -> x0, waiting for transfers between devices: 90.3 us -> none  [per_device(): grad_total = lax.psum(group_grad, 'replica')]
    dot_general x54 -> x0, matrix products: 83.4 us -> none  [the longest x6 12.9 us: head_grads(): jnp.einsum('xuc,xlc->xul', gradient_masked, value_block_rows, preferred_e...]
    ppermute x0 -> x29, waiting for transfers between devices: none -> 80 us  [the longest x19 58.7 us: swap(): return lax.ppermute(a, 'group', [(i, i ^ bit) for i in range(4)])]
    all_gather x1 -> x0, other arithmetic: 78.3 us -> none  [per_device(): gathered = lax.all_gather(shard_low, 'group', axis=0, tiled=True)]
    unnamed x9 -> x0, waiting for transfers between devices: 73.7 us -> none
    all_gather x3 -> x0, waiting for transfers between devices: 69.8 us -> none  [the longest x1 51.8 us: per_device(): gathered = lax.all_gather(shard_low, 'group', axis=0, tiled=True)]
    concatenate x1 -> x0, local copies, waits for them, and re-layouts: 50.5 us -> none  [per_device(): jnp.concatenate([member.reshape(-1) for member in (d_w_qkv, d_w_out, d_w_...]
  transfers between devices with their start and end apart: 7 -> 29, of which waited for: 4 -> 18; matrix products, arithmetic and copies ran while one was open for 17% -> 9% of each run, Pallas kernels for 0% -> 9%
where the time goes in v1:
time: 204 us; the launch traced here: 202 us
  waiting for transfers between devices  80 us (39%)
  Pallas kernels  43.9 us (22%)
  other arithmetic  35.4 us (17%)
  starting transfers between devices  32.2 us (16%)
  local copies, waits for them, and re-layouts  8.55 us (4%)
  between operations  2.37 us (1%)
    ppermute x19, waiting for transfers between devices, swap(): return lax.ppermute(a, 'group', [(i, i ^ bit) for i in range(4)])  58.7 us
    ppermute x10, waiting for transfers between devices, swap_rep(): return lax.ppermute(a, 'replica', [(i, i ^ bit) for i in range(replicas)])  21.2 us
    pallas_call x1, Pallas kernels, per_device(): pl.pallas_call(attend_back_kernel, out_shape=(shape(PAD_B, 128), shape(ro...  18.4 us
    ppermute x10, starting transfers between devices, swap_rep(): return lax.ppermute(a, 'replica', [(i, i ^ bit) for i in range(replicas)])  16.5 us
    ppermute x19, starting transfers between devices, swap(): return lax.ppermute(a, 'group', [(i, i ^ bit) for i in range(4)])  15.7 us
    pallas_call x1, Pallas kernels, per_device(): pl.pallas_call(qkv_attend_kernel, out_shape=(shape(2 * rows, D), shape(D,...  14.4 us
    select_n x8, other arithmetic, reduce_all(): jnp.where(side == 0, jnp.concatenate([part, got]), jnp.concatenate([got,...  12.4 us
    pallas_call x1, Pallas kernels, per_device(): pl.pallas_call(mlp_kernel, out_shape=(shape(rows, D), shape(rows, D, dtyp...  11.1 us
  transfers between devices with their start and end apart: 29, of which 18 were waited for; matrix products, arithmetic and copies ran while one was open for 9% of the time, Pallas kernels for 9%

profile of v1, /device:TPU:0, one launch (start us, length us, event | category | flops | bytes accessed | tf_op | source)
XLA Modules:
  0.0 202.4 jit_solution(15716903599715103571)
XLA Ops:
  0.6 1.6 convert_bitcast_fusion.1
  2.3 0.6 collective-permute-start.2
  2.8 2.1 %collective-permute-done.2 = bf16[3488,128]{1,0:T(8,128)(2,1)S(1)} collective-permute-done((bf16[3488,128]{1,0:T(8,128)(2,1)S(1)}, bf16[3488,128]{1,0:T(8,128)(2,1)S(1)}, u32[]{:S(2)}, u32[]{:S(2)}) %collective-permute-start.2) | collective-permute-done | bytes 892960 | tf_op jit(solution)/shard_map/ppermute | solution.py:343
  4.9 1.1 broadcast_select_fusion.6
  6.0 2.8 %collective-permute-start.3 = (bf16[1744,128]{1,0:T(8,128)(2,1)S(1)}, bf16[1744,128]{1,0:T(8,128)(2,1)S(1)}, u32[]{:S(2)}, u32[]{:S(2)}) collective-permute-start(bf16[1744,128]{1,0:T(8,128)(2,1)S(1)} %get-tuple-element.52), channel_id=1, source_target_pairs={{0,16},{8,24},{16,0},{24,8},{1,17},{9,25},{17,1},{25,9},{2,18},{10... | collective-permute-start | bytes 1339400 | tf_op jit(solution)/shard_map/ppermute | solution.py:343
  8.8 11.1 %collective-permute-done.3 = bf16[1744,128]{1,0:T(8,128)(2,1)S(1)} collective-permute-done((bf16[1744,128]{1,0:T(8,128)(2,1)S(1)}, bf16[1744,128]{1,0:T(8,128)(2,1)S(1)}, u32[]{:S(2)}, u32[]{:S(2)}) %collective-permute-start.3) | collective-permute-done | bytes 446496 | tf_op jit(solution)/shard_map/ppermute | solution.py:343
  19.9 0.7 dynamic-slice_bitcast_fusion.3
  20.6 2.0 collective-permute-start
  22.7 1.1 dynamic-slice_bitcast_fusion.1
  23.8 9.9 %collective-permute-done = bf16[256,384]{1,0:T(8,128)(2,1)S(1)} collective-permute-done((bf16[256,384]{1,0:T(8,128)(2,1)}, bf16[256,384]{1,0:T(8,128)(2,1)S(1)}, u32[]{:S(2)}, u32[]{:S(2)}) %collective-permute-start) | collective-permute-done | bytes 196640 | tf_op jit(solution)/shard_map/ppermute | solution.py:343
  33.8 3.6 %collective-permute-done.5 = bf16[256,384]{1,0:T(8,128)(2,1)} collective-permute-done((bf16[256,384]{1,0:T(8,128)(2,1)S(1)}, bf16[256,384]{1,0:T(8,128)(2,1)}, u32[]{:S(2)}, u32[]{:S(2)}) %collective-permute-start.5) | collective-permute-done | bytes 196640 | tf_op jit(solution)/shard_map/ppermute | solution.py:343
  37.5 1.7 pad_maximum_fusion.3.cot_ref
  39.2 1.8 broadcast_select_fusion.4
  41.0 1.9 broadcast_select_fusion.2
  43.0 1.0 slice.36.wf_ref
  43.9 0.6 slice.37.vec_ref
  44.5 0.7 copy-done.7
  45.3 14.4 %qkv_attend.1 = (bf16[1024,384]{1,0:T(8,128)(2,1)}, bf16[384,1152]{1,0:T(8,128)(2,1)}, bf16[6,512,128]{2,1,0:T(8,128)(2,1)}, bf16[3,1024,128]{2,1,0:T(8,128)(2,1...) custom-call(bf16[512,384]{1,0:T(8,128)(2,1)} %copy-done.3, ...), custom_call_target="tpu_custom_call" | custom-call | tf_op jit(solution)/shard_map/qkv_attend/pallas_call | solution.py:377
  59.7 11.1 %mlp.1 = (bf16[512,384]{1,0:T(8,128)(2,1)}, f32[512,384]{1,0:T(8,128)}, bf16[512,384]{1,0:T(8,128)(2,1)}, bf16[10496,128]{1,0:T(8,128)(2,1)}, f32[24,128]{1,0:T(8,128)}) custom-call(bf16[512,384]{1,0:T(8,128)(2,1)} %copy-done.3, f32[3,512,128]{2,1,0:T(8,128)} %get-tuple-element.25.o_ref.out_ref, bf16[512,384]{1,0:T(8,128)(2,1)} %pad_maximum_fusion.3.cot_ref, ...), custom_call_target="tpu_custom_call" | custom-call | tf_op jit(solution)/shard_map/mlp/pallas_call | solution.py:389
  70.8 1.4 constant_dynamic-slice_fusion.3
  72.2 0.6 collective-permute-start.20
  72.7 2.7 %collective-permute-done.20 = bf16[5248,128]{1,0:T(8,128)(2,1)S(1)} collective-permute-done((bf16[5248,128]{1,0:T(8,128)(2,1)S(1)}, bf16[5248,128]{1,0:T(8,128)(2,1)S(1)}, u32[]{:S(2)}, u32[]{:S(2)}) %collective-permute-start.20) | collective-permute-done | bytes 1343520 | tf_op jit(solution)/shard_map/ppermute | solution.py:343
  75.5 1.7 add_convert_fusion
  77.2 1.8 collective-permute-start.21
  79.0 15.6 %collective-permute-done.21 = bf16[2624,128]{1,0:T(8,128)(2,1)S(1)} collective-permute-done((bf16[2624,128]{1,0:T(8,128)(2,1)S(1)}, bf16[2624,128]{1,0:T(8,128)(2,1)S(1)}, u32[]{:S(2)}, u32[]{:S(2)}) %collective-permute-start.21) | collective-permute-done | bytes 671776 | tf_op jit(solution)/shard_map/ppermute | solution.py:343
  94.6 0.2 add_convert_fusion.1
  94.8 1.8 collective-permute-start.22
  96.7 18.4 %attend_back.1 = (bf16[3584,128]{1,0:T(8,128)(2,1)}, f32[512,384]{1,0:T(8,128)}, bf16[512,384]{1,0:T(8,128)(2,1)}) custom-call(bf16[512,384]{1,0:T(8,128)(2,1)} %copy-done.3, bf16[512,384]{1,0:T(8,128)(2,1)} %copy-done.7, bf16[1024,384]{1,0:T(8,128)(2,1)} %get-tuple-element.27.act_ref, bf16[384,1152]{1,0:T(8,128)(2,1)} %get-tuple-element.28.w2_ref, ...), custom_call_target="tpu_custom_call" | custom-call | tf_op jit(solution)/shard_map/attend_back/pallas_call | solution.py:402
  115.1 1.1 constant_dynamic-slice_fusion.7
  116.5 1.6 collective-permute-start.23
  118.3 1.6 collective-permute-start.12
  119.9 3.4 %collective-permute-done.23 = bf16[656,128]{1,0:T(8,128)(2,1)S(1)} collective-permute-done((bf16[656,128]{1,0:T(8,128)(2,1)S(1)}, bf16[656,128]{1,0:T(8,128)(2,1)S(1)}, u32[]{:S(2)}, u32[]{:S(2)}) %collective-permute-start.23) | collective-permute-done | bytes 167968 | tf_op jit(solution)/shard_map/ppermute | solution.py:346
  123.3 2.7 %collective-permute-start.24 = (bf16[656,128]{1,0:T(8,128)(2,1)S(1)}, bf16[656,128]{1,0:T(8,128)(2,1)S(1)}, u32[]{:S(2)}, u32[]{:S(2)}) collective-permute-start(bf16[656,128]{1,0:T(8,128)(2,1)S(1)} %add_convert_fusion.7), channel_id=1, source_target_pairs={{0,4},{1,5},{2,6},{3,7},{4,0},{5,1},{6,2},{7,3},{8,12},{9,13},{10,... | collective-permute-start | bytes 503816 | tf_op jit(solution)/shard_map/ppermute | solution.py:346
  125.9 0.1 collective-permute-done.12
  126.2 0.6 collective-permute-start.13
  126.7 6.9 %collective-permute-done.24 = bf16[656,128]{1,0:T(8,128)(2,1)S(1)} collective-permute-done((bf16[656,128]{1,0:T(8,128)(2,1)S(1)}, bf16[656,128]{1,0:T(8,128)(2,1)S(1)}, u32[]{:S(2)}, u32[]{:S(2)}) %collective-permute-start.24) | collective-permute-done | bytes 167968 | tf_op jit(solution)/shard_map/ppermute | solution.py:346
  133.7 0.7 collective-permute-start.25
  134.5 4.6 %collective-permute-done.25 = bf16[656,128]{1,0:T(8,128)(2,1)S(1)} collective-permute-done((bf16[656,128]{1,0:T(8,128)(2,1)S(1)}, bf16[656,128]{1,0:T(8,128)(2,1)S(1)}, u32[]{:S(2)}, u32[]{:S(2)}) %collective-permute-start.25) | collective-permute-done | bytes 167968 | tf_op jit(solution)/shard_map/ppermute | solution.py:346
  139.2 0.5 collective-permute-start.26
  139.8 1.6 collective-permute-start.14
  141.3 2.6 %collective-permute-done.14 = bf16[224,128]{1,0:T(8,128)(2,1)S(1)} collective-permute-done((bf16[224,128]{1,0:T(8,128)(2,1)S(1)}, bf16[224,128]{1,0:T(8,128)(2,1)S(1)}, u32[]{:S(2)}, u32[]{:S(2)}) %collective-permute-start.14) | collective-permute-done | bytes 57376 | tf_op jit(solution)/shard_map/ppermute | solution.py:346
  144.0 3.3 %collective-permute-start.15 = (bf16[224,128]{1,0:T(8,128)(2,1)S(1)}, bf16[224,128]{1,0:T(8,128)(2,1)S(1)}, u32[]{:S(2)}, u32[]{:S(2)}) collective-permute-start(bf16[224,128]{1,0:T(8,128)(2,1)S(1)} %add_convert_fusion.10), channel_id=1, source_target_pairs={{0,4},{1,5},{2,6},{3,7},{4,0},{5,1},{6,2},{7,3},{8,12},{9,13},{10,... | collective-permute-start | bytes 172040 | tf_op jit(solution)/shard_map/ppermute | solution.py:346
  147.3 0.2 maximum_select_fusion.4
  147.5 1.6 collective-permute-start.27
  149.0 0.4 collective-permute-done.15
  149.4 2.2 %collective-permute-start.16 = (bf16[224,128]{1,0:T(8,128)(2,1)S(1)}, bf16[224,128]{1,0:T(8,128)(2,1)S(1)}, u32[]{:S(2)}, u32[]{:S(2)}) collective-permute-start(bf16[224,128]{1,0:T(8,128)(2,1)S(1)} %add_convert_fusion.9), channel_id=1, source_target_pairs={{0,2},{1,3},{2,0},{3,1},{4,6},{5,7},{6,4},{7,5},{8,10},{9,11},{10,... | collective-permute-start | bytes 172040 | tf_op jit(solution)/shard_map/ppermute | solution.py:346
  151.6 2.2 %collective-permute-done.16 = bf16[224,128]{1,0:T(8,128)(2,1)S(1)} collective-permute-done((bf16[224,128]{1,0:T(8,128)(2,1)S(1)}, bf16[224,128]{1,0:T(8,128)(2,1)S(1)}, u32[]{:S(2)}, u32[]{:S(2)}) %collective-permute-start.16) | collective-permute-done | bytes 57376 | tf_op jit(solution)/shard_map/ppermute | solution.py:346
  153.8 1.5 collective-permute-start.17
  155.3 0.7 slice_bitcast_fusion.1
  156.0 1.5 collective-permute-start.8
  157.5 1.2 collective-permute-done.17
  158.7 1.5 collective-permute-start.18
  160.2 5.3 %collective-permute-done.27 = bf16[2624,128]{1,0:T(8,128)(2,1)S(1)} collective-permute-done((bf16[2624,128]{1,0:T(8,128)(2,1)S(1)}, bf16[2624,128]{1,0:T(8,128)(2,1)S(1)}, u32[]{:S(2)}, u32[]{:S(2)}) %collective-permute-start.27) | collective-permute-done | bytes 671776 | tf_op jit(solution)/shard_map/ppermute | solution.py:343
  165.5 0.3 maximum_select_fusion
  166.0 5.3 %collective-permute-done.18 = bf16[896,128]{1,0:T(8,128)(2,1)S(1)} collective-permute-done((bf16[896,128]{1,0:T(8,128)(2,1)S(1)}, bf16[896,128]{1,0:T(8,128)(2,1)S(1)}, u32[]{:S(2)}, u32[]{:S(2)}) %collective-permute-start.18) | collective-permute-done | bytes 229408 | tf_op jit(solution)/shard_map/ppermute | solution.py:343
  171.5 0.7 slice_bitcast_fusion
  172.3 1.5 collective-permute-start.10
  175.1 1.8 maximum_select_fusion.6
  176.9 2.9 %collective-permute-done.10 = bf16[256,384]{1,0:T(8,128)(2,1)} collective-permute-done((bf16[256,384]{1,0:T(8,128)(2,1)}, bf16[256,384]{1,0:T(8,128)(2,1)}, u32[]{:S(2)}, u32[]{:S(2)}) %collective-permute-start.10) | collective-permute-done | bytes 196640 | tf_op jit(solution)/shard_map/ppermute | solution.py:343
  179.9 1.8 maximum_select_fusion.7
  181.7 1.4 maximum_select_fusion.1
  183.2 10.2 %fusion = bf16[10368,128]{1,0:T(8,128)(2,1)S(1)} fusion(bf16[5248,128]{1,0:T(8,128)(2,1)S(1)} %collective-permute-done.28, bf16[5248,128]{1,0:T(8,128)(2,1)S(1)} %maximum_select_fusion, pred[]{:T(512)S(6)} %eq.15), kind=kLoop, calls=%fused_computation.5 | loop fusion | flops 11943936 | bytes 5341185 | tf_op jit(solution)/shard_map/jit(_where)/select_n | solution.py:438
  193.4 7.1 %fusion.3 = (bf16[443648]{0:T(1024)(128)(2,1)}, f32[443648]{0:T(1024)S(1)}, f32[443648]{0:T(1024)}, f32[443648]{0:T(1024)}) fusion(f32[443648]{0:T(1024)S(1)} %copy-done.2, f32[]{:T(128)} %bitcast.21, f32[443648]{0:T(1024)S(1)} %copy-done.5, s32[]{:T(128)S(6)} %select_n.267, bf16[40,128]{1,0:T(8,128)(2,1)S(1)} %slice.41, bf16[10368,128]{1,0:T(8,128)(2,1)S(1)} %fusion, ...), kind=kLoop, calls=%fused_computation.59 | loop fusion | flops 5767424 | bytes 13309448 | tf_op jit(solution)/shard_map/convert_element_type | solution.py:451
  200.6 1.7 multiply_add_fusion
  (69 shorter events, 1.8 us)
Async XLA Ops:
  2.2 17.7 %copy-start.10 = (bf16[2,256,384]{2,1,0:T(8,128)(2,1)S(1)}, bf16[2,256,384]{2,1,0:T(8,128)(2,1)}, u32[]{:S(2)}) copy-start(bf16[2,256,384]{2,1,0:T(8,128)(2,1)} %param.7) | copy-start | bytes 1179652
  2.3 2.6 %collective-permute-start.2 = (bf16[3488,128]{1,0:T(8,128)(2,1)S(1)}, bf16[3488,128]{1,0:T(8,128)(2,1)S(1)}, u32[]{:S(2)}, u32[]{:S(2)}) collective-permute-start(bf16[3488,128]{1,0:T(8,128)(2,1)S(1)} %pad.4), channel_id=1, source_target_pairs={{0,8},{8,0},{16,24},{24,16},{1,9},{9,1},{17,25},{25,17},{2,10},{10... | collective-permute-start | bytes 2678792 | tf_op jit(solution)/shard_map/ppermute | solution.py:343
  6.0 14.0 %collective-permute-start.3 = (bf16[1744,128]{1,0:T(8,128)(2,1)S(1)}, bf16[1744,128]{1,0:T(8,128)(2,1)S(1)}, u32[]{:S(2)}, u32[]{:S(2)}) collective-permute-start(bf16[1744,128]{1,0:T(8,128)(2,1)S(1)} %get-tuple-element.52), channel_id=1, source_target_pairs={{0,16},{8,24},{16,0},{24,8},{1,17},{9,25},{17,1},{25,9},{2,18},{10... | collective-permute-start | bytes 1339400 | tf_op jit(solution)/shard_map/ppermute | solution.py:343
  8.8 30.4 %collective-permute-start.6 = (bf16[1744,128]{1,0:T(8,128)(2,1)}, bf16[1744,128]{1,0:T(8,128)(2,1)S(1)}, u32[]{:S(2)}, u32[]{:S(2)}) collective-permute-start(bf16[1744,128]{1,0:T(8,128)(2,1)} %get-tuple-element.51), channel_id=1, source_target_pairs={{0,16},{8,24},{16,0},{24,8},{1,17},{9,25},{17,1},{25,9},{2,18},{10... | collective-permute-start | bytes 1339400 | tf_op jit(solution)/shard_map/ppermute | solution.py:343
  19.9 19.3 %collective-permute-start.4 = (bf16[1744,128]{1,0:T(8,128)(2,1)S(1)}, bf16[1744,128]{1,0:T(8,128)(2,1)}, u32[]{:S(2)}, u32[]{:S(2)}) collective-permute-start(bf16[1744,128]{1,0:T(8,128)(2,1)S(1)} %collective-permute-done.3), channel_id=1, source_target_pairs={{0,8},{8,0},{16,24},{24,16},{1,9},{9,1},{17,25},{25,17},{2,10},{10... | collective-permute-start | bytes 1339400 | tf_op jit(solution)/shard_map/ppermute | solution.py:343
  20.6 13.1 %collective-permute-start = (bf16[256,384]{1,0:T(8,128)(2,1)}, bf16[256,384]{1,0:T(8,128)(2,1)S(1)}, u32[]{:S(2)}, u32[]{:S(2)}) collective-permute-start(bf16[256,384]{1,0:T(8,128)(2,1)} %get-tuple-element.60), channel_id=1, source_target_pairs={{0,16},{8,24},{16,0},{24,8},{1,17},{9,25},{17,1},{25,9},{2,18},{10... | collective-permute-start | bytes 589832 | tf_op jit(solution)/shard_map/ppermute | solution.py:343
  23.7 13.7 %collective-permute-start.5 = (bf16[256,384]{1,0:T(8,128)(2,1)S(1)}, bf16[256,384]{1,0:T(8,128)(2,1)}, u32[]{:S(2)}, u32[]{:S(2)}) collective-permute-start(bf16[256,384]{1,0:T(8,128)(2,1)S(1)} %get-tuple-element.58), channel_id=1, source_target_pairs={{0,16},{8,24},{16,0},{24,8},{1,17},{9,25},{17,1},{25,9},{2,18},{10... | collective-permute-start | bytes 589832 | tf_op jit(solution)/shard_map/ppermute | solution.py:343
  33.7 7.2 %copy-start.3 = (bf16[512,384]{1,0:T(8,128)(2,1)}, bf16[512,384]{1,0:T(8,128)(2,1)S(1)}, u32[]{:S(2)}) copy-start(bf16[512,384]{1,0:T(8,128)(2,1)S(1)} %pad_maximum_fusion.2.xo_ref.x_ref) | copy-start | bytes 1179652
  33.8 10.8 %collective-permute-start.1 = (bf16[512,384]{1,0:T(8,128)(2,1)S(1)}, bf16[512,384]{1,0:T(8,128)(2,1)S(1)}, u32[]{:S(2)}, u32[]{:S(2)}) collective-permute-start(bf16[512,384]{1,0:T(8,128)(2,1)S(1)} %pad_maximum_fusion.2.xo_ref.x_ref), channel_id=1, source_target_pairs={{0,8},{8,0},{16,24},{24,16},{1,9},{9,1},{17,25},{25,17},{2,10},{10... | collective-permute-start | bytes 1179656 | tf_op jit(solution)/shard_map/ppermute | solution.py:343
  39.2 1.8 collective-permute-start.7
  41.0 2.0 copy-start
  41.0 2.9 %copy-start.4 = (bf16[3488,128]{1,0:T(8,128)(2,1)}, bf16[3488,128]{1,0:T(8,128)(2,1)S(1)}, u32[]{:S(2)}) copy-start(bf16[3488,128]{1,0:T(8,128)(2,1)S(1)} %get-tuple-element.49.q3_ref) | copy-start | bytes 2678788
  44.5 0.7 copy-start.7
  72.2 3.3 %collective-permute-start.20 = (bf16[5248,128]{1,0:T(8,128)(2,1)S(1)}, bf16[5248,128]{1,0:T(8,128)(2,1)S(1)}, u32[]{:S(2)}, u32[]{:S(2)}) collective-permute-start(bf16[5248,128]{1,0:T(8,128)(2,1)S(1)} %constant_dynamic-slice_fusion.3), channel_id=1, source_target_pairs={{0,8},{8,0},{16,24},{24,16},{1,9},{9,1},{17,25},{25,17},{2,10},{10... | collective-permute-start | bytes 4030472 | tf_op jit(solution)/shard_map/ppermute | solution.py:343
  77.2 17.4 %collective-permute-start.21 = (bf16[2624,128]{1,0:T(8,128)(2,1)S(1)}, bf16[2624,128]{1,0:T(8,128)(2,1)S(1)}, u32[]{:S(2)}, u32[]{:S(2)}) collective-permute-start(bf16[2624,128]{1,0:T(8,128)(2,1)S(1)} %constant_dynamic-slice_fusion.2), channel_id=1, source_target_pairs={{0,16},{8,24},{16,0},{24,8},{1,17},{9,25},{17,1},{25,9},{2,18},{10... | collective-permute-start | bytes 2015240 | tf_op jit(solution)/shard_map/ppermute | solution.py:343
  94.8 21.5 %collective-permute-start.22 = (bf16[1312,128]{1,0:T(8,128)(2,1)S(1)}, bf16[1312,128]{1,0:T(8,128)(2,1)S(1)}, u32[]{:S(2)}, u32[]{:S(2)}) collective-permute-start(bf16[1312,128]{1,0:T(8,128)(2,1)S(1)} %constant_dynamic-slice_fusion.1), channel_id=1, source_target_pairs={{0,1},{1,0},{2,3},{3,2},{4,5},{5,4},{6,7},{7,6},{8,9},{9,8},{10,11... | collective-permute-start | bytes 1007624 | tf_op jit(solution)/shard_map/ppermute | solution.py:346
  115.1 3.0 %copy-start.8 = (bf16[3584,128]{1,0:T(8,128)(2,1)S(1)}, bf16[3584,128]{1,0:T(8,128)(2,1)}, u32[]{:S(2)}) copy-start(bf16[3584,128]{1,0:T(8,128)(2,1)} %get-tuple-element.41) | copy-start | bytes 2752516
  116.3 1.9 collective-permute-start.11
  116.5 6.7 %collective-permute-start.23 = (bf16[656,128]{1,0:T(8,128)(2,1)S(1)}, bf16[656,128]{1,0:T(8,128)(2,1)S(1)}, u32[]{:S(2)}, u32[]{:S(2)}) collective-permute-start(bf16[656,128]{1,0:T(8,128)(2,1)S(1)} %constant_dynamic-slice_fusion), channel_id=1, source_target_pairs={{0,2},{1,3},{2,0},{3,1},{4,6},{5,7},{6,4},{7,5},{8,10},{9,11},{10,... | collective-permute-start | bytes 503816 | tf_op jit(solution)/shard_map/ppermute | solution.py:346
  118.3 7.8 %collective-permute-start.12 = (bf16[896,128]{1,0:T(8,128)(2,1)S(1)}, bf16[896,128]{1,0:T(8,128)(2,1)S(1)}, u32[]{:S(2)}, u32[]{:S(2)}) collective-permute-start(bf16[896,128]{1,0:T(8,128)(2,1)S(1)} %constant_dynamic-slice_fusion.6), channel_id=1, source_target_pairs={{0,16},{8,24},{16,0},{24,8},{1,17},{9,25},{17,1},{25,9},{2,18},{10... | collective-permute-start | bytes 688136 | tf_op jit(solution)/shard_map/ppermute | solution.py:343
  123.3 10.4 %collective-permute-start.24 = (bf16[656,128]{1,0:T(8,128)(2,1)S(1)}, bf16[656,128]{1,0:T(8,128)(2,1)S(1)}, u32[]{:S(2)}, u32[]{:S(2)}) collective-permute-start(bf16[656,128]{1,0:T(8,128)(2,1)S(1)} %add_convert_fusion.7), channel_id=1, source_target_pairs={{0,4},{1,5},{2,6},{3,7},{4,0},{5,1},{6,2},{7,3},{8,12},{9,13},{10,... | collective-permute-start | bytes 503816 | tf_op jit(solution)/shard_map/ppermute | solution.py:346
  126.1 25.5 %copy-start.12 = (bf16[512,384]{1,0:T(8,128)(2,1)S(1)}, bf16[512,384]{1,0:T(8,128)(2,1)}, u32[]{:S(2)}) copy-start(bf16[512,384]{1,0:T(8,128)(2,1)} %get-tuple-element.40) | copy-start | bytes 1179652
  126.2 29.1 %copy-start.11 = (bf16[512,384]{1,0:T(8,128)(2,1)S(1)}, bf16[512,384]{1,0:T(8,128)(2,1)}, u32[]{:S(2)}) copy-start(bf16[512,384]{1,0:T(8,128)(2,1)} %get-tuple-element.26) | copy-start | bytes 1179652
  126.2 8.3 %collective-permute-start.13 = (bf16[448,128]{1,0:T(8,128)(2,1)S(1)}, bf16[448,128]{1,0:T(8,128)(2,1)S(1)}, u32[]{:S(2)}, u32[]{:S(2)}) collective-permute-start(bf16[448,128]{1,0:T(8,128)(2,1)S(1)} %constant_dynamic-slice_fusion.5), channel_id=1, source_target_pairs={{0,1},{1,0},{2,3},{3,2},{4,5},{5,4},{6,7},{7,6},{8,9},{9,8},{10,11... | collective-permute-start | bytes 344072 | tf_op jit(solution)/shard_map/ppermute | solution.py:346
  133.7 5.4 %collective-permute-start.25 = (bf16[656,128]{1,0:T(8,128)(2,1)S(1)}, bf16[656,128]{1,0:T(8,128)(2,1)S(1)}, u32[]{:S(2)}, u32[]{:S(2)}) collective-permute-start(bf16[656,128]{1,0:T(8,128)(2,1)S(1)} %add_convert_fusion.6), channel_id=1, source_target_pairs={{0,2},{1,3},{2,0},{3,1},{4,6},{5,7},{6,4},{7,5},{8,10},{9,11},{10,... | collective-permute-start | bytes 503816 | tf_op jit(solution)/shard_map/ppermute | solution.py:346
  139.2 8.1 %collective-permute-start.26 = (bf16[1312,128]{1,0:T(8,128)(2,1)S(1)}, bf16[1312,128]{1,0:T(8,128)(2,1)S(1)}, u32[]{:S(2)}, u32[]{:S(2)}) collective-permute-start(bf16[1312,128]{1,0:T(8,128)(2,1)S(1)} %maximum_select_fusion.8), channel_id=1, source_target_pairs={{0,1},{1,0},{2,3},{3,2},{4,5},{5,4},{6,7},{7,6},{8,9},{9,8},{10,11... | collective-permute-start | bytes 1007624 | tf_op jit(solution)/shard_map/ppermute | solution.py:346
  139.8 4.2 %collective-permute-start.14 = (bf16[224,128]{1,0:T(8,128)(2,1)S(1)}, bf16[224,128]{1,0:T(8,128)(2,1)S(1)}, u32[]{:S(2)}, u32[]{:S(2)}) collective-permute-start(bf16[224,128]{1,0:T(8,128)(2,1)S(1)} %constant_dynamic-slice_fusion.4), channel_id=1, source_target_pairs={{0,2},{1,3},{2,0},{3,1},{4,6},{5,7},{6,4},{7,5},{8,10},{9,11},{10,... | collective-permute-start | bytes 172040 | tf_op jit(solution)/shard_map/ppermute | solution.py:346
  144.0 5.4 %collective-permute-start.15 = (bf16[224,128]{1,0:T(8,128)(2,1)S(1)}, bf16[224,128]{1,0:T(8,128)(2,1)S(1)}, u32[]{:S(2)}, u32[]{:S(2)}) collective-permute-start(bf16[224,128]{1,0:T(8,128)(2,1)S(1)} %add_convert_fusion.10), channel_id=1, source_target_pairs={{0,4},{1,5},{2,6},{3,7},{4,0},{5,1},{6,2},{7,3},{8,12},{9,13},{10,... | collective-permute-start | bytes 172040 | tf_op jit(solution)/shard_map/ppermute | solution.py:346
  147.5 18.0 %collective-permute-start.27 = (bf16[2624,128]{1,0:T(8,128)(2,1)S(1)}, bf16[2624,128]{1,0:T(8,128)(2,1)S(1)}, u32[]{:S(2)}, u32[]{:S(2)}) collective-permute-start(bf16[2624,128]{1,0:T(8,128)(2,1)S(1)} %maximum_select_fusion.4), channel_id=1, source_target_pairs={{0,16},{8,24},{16,0},{24,8},{1,17},{9,25},{17,1},{25,9},{2,18},{10... | collective-permute-start | bytes 2015240 | tf_op jit(solution)/shard_map/ppermute | solution.py:343
  149.4 4.3 %collective-permute-start.16 = (bf16[224,128]{1,0:T(8,128)(2,1)S(1)}, bf16[224,128]{1,0:T(8,128)(2,1)S(1)}, u32[]{:S(2)}, u32[]{:S(2)}) collective-permute-start(bf16[224,128]{1,0:T(8,128)(2,1)S(1)} %add_convert_fusion.9), channel_id=1, source_target_pairs={{0,2},{1,3},{2,0},{3,1},{4,6},{5,7},{6,4},{7,5},{8,10},{9,11},{10,... | collective-permute-start | bytes 172040 | tf_op jit(solution)/shard_map/ppermute | solution.py:346
  151.6 14.3 %collective-permute-start.9 = (bf16[512,384]{1,0:T(8,128)(2,1)S(1)}, bf16[512,384]{1,0:T(8,128)(2,1)S(1)}, u32[]{:S(2)}, u32[]{:S(2)}) collective-permute-start(bf16[512,384]{1,0:T(8,128)(2,1)S(1)} %copy-done.12), channel_id=1, source_target_pairs={{0,8},{8,0},{16,24},{24,16},{1,9},{9,1},{17,25},{25,17},{2,10},{10... | collective-permute-start | bytes 1179656 | tf_op jit(solution)/shard_map/ppermute | solution.py:343
  153.8 4.9 %collective-permute-start.17 = (bf16[448,128]{1,0:T(8,128)(2,1)S(1)}, bf16[448,128]{1,0:T(8,128)(2,1)S(1)}, u32[]{:S(2)}, u32[]{:S(2)}) collective-permute-start(bf16[448,128]{1,0:T(8,128)(2,1)S(1)} %maximum_select_fusion.10), channel_id=1, source_target_pairs={{0,1},{1,0},{2,3},{3,2},{4,5},{5,4},{6,7},{7,6},{8,9},{9,8},{10,11... | collective-permute-start | bytes 344072 | tf_op jit(solution)/shard_map/ppermute | solution.py:346
  155.3 10.7 %copy-start.9 = (f32[512,384]{1,0:T(8,128)S(1)}, f32[512,384]{1,0:T(8,128)}, u32[]{:S(2)}) copy-start(f32[512,384]{1,0:T(8,128)} %get-tuple-element.39) | copy-start | bytes 2359300
  156.0 19.1 %collective-permute-start.8 = (bf16[256,384]{1,0:T(8,128)(2,1)}, bf16[256,384]{1,0:T(8,128)(2,1)}, u32[]{:S(2)}, u32[]{:S(2)}) collective-permute-start(bf16[256,384]{1,0:T(8,128)(2,1)} %get-tuple-element.56), channel_id=1, source_target_pairs={{0,16},{8,24},{16,0},{24,8},{1,17},{9,25},{17,1},{25,9},{2,18},{10... | collective-permute-start | bytes 589832 | tf_op jit(solution)/shard_map/ppermute | solution.py:343
  158.7 12.6 %collective-permute-start.18 = (bf16[896,128]{1,0:T(8,128)(2,1)S(1)}, bf16[896,128]{1,0:T(8,128)(2,1)S(1)}, u32[]{:S(2)}, u32[]{:S(2)}) collective-permute-start(bf16[896,128]{1,0:T(8,128)(2,1)S(1)} %maximum_select_fusion.9), channel_id=1, source_target_pairs={{0,16},{8,24},{16,0},{24,8},{1,17},{9,25},{17,1},{25,9},{2,18},{10... | collective-permute-start | bytes 688136 | tf_op jit(solution)/shard_map/ppermute | solution.py:343
  165.8 17.4 %collective-permute-start.28 = (bf16[5248,128]{1,0:T(8,128)(2,1)S(1)}, bf16[5248,128]{1,0:T(8,128)(2,1)S(1)}, u32[]{:S(2)}, u32[]{:S(2)}) collective-permute-start(bf16[5248,128]{1,0:T(8,128)(2,1)S(1)} %maximum_select_fusion), channel_id=1, source_target_pairs={{0,8},{8,0},{16,24},{24,16},{1,9},{9,1},{17,25},{25,17},{2,10},{10... | collective-permute-start | bytes 4030472 | tf_op jit(solution)/shard_map/ppermute | solution.py:343
  171.5 10.3 %collective-permute-start.19 = (bf16[1792,128]{1,0:T(8,128)(2,1)S(1)}, bf16[1792,128]{1,0:T(8,128)(2,1)}, u32[]{:S(2)}, u32[]{:S(2)}) collective-permute-start(bf16[1792,128]{1,0:T(8,128)(2,1)S(1)} %maximum_select_fusion.5), channel_id=1, source_target_pairs={{0,8},{8,0},{16,24},{24,16},{1,9},{9,1},{17,25},{25,17},{2,10},{10... | collective-permute-start | bytes 1376264 | tf_op jit(solution)/shard_map/ppermute | solution.py:343
  172.3 7.6 %collective-permute-start.10 = (bf16[256,384]{1,0:T(8,128)(2,1)}, bf16[256,384]{1,0:T(8,128)(2,1)}, u32[]{:S(2)}, u32[]{:S(2)}) collective-permute-start(bf16[256,384]{1,0:T(8,128)(2,1)} %get-tuple-element.54), channel_id=1, source_target_pairs={{0,16},{8,24},{16,0},{24,8},{1,17},{9,25},{17,1},{25,9},{2,18},{10... | collective-permute-start | bytes 589832 | tf_op jit(solution)/shard_map/ppermute | solution.py:343
  183.2 10.2 %copy-start.2 = (f32[443648]{0:T(1024)S(1)}, f32[443648]{0:T(1024)}, u32[]{:S(2)}) copy-start(f32[443648]{0:T(1024)} %param.9) | copy-start | bytes 5323780
  183.2 10.2 %copy-start.5 = (f32[443648]{0:T(1024)S(1)}, f32[443648]{0:T(1024)}, u32[]{:S(2)}) copy-start(f32[443648]{0:T(1024)} %param.10) | copy-start | bytes 5323780
  193.4 7.2 %copy-start.6 = (f32[443648]{0:T(1024)S(1)}, f32[443648]{0:T(1024)}, u32[]{:S(2)}) copy-start(f32[443648]{0:T(1024)} %param.11) | copy-start | bytes 5323780
  200.6 1.8 copy-start.1

commit v2 on v1

v2 whole, which is shorter than its diff:
```python
import jax
import jax.numpy as jnp
from jax import lax
from jax.experimental import pallas as pl
from jax.experimental.pallas import tpu as pltpu
from jax.sharding import PartitionSpec as P


D = 384
DH = 64
FF = 1536
EPSILON = 1e-06
MOMENT = 0.9
DECAY_MAX = 0.999
INV_ROOT_TWO = 0.7071067811865476
INV_ROOT_TAU = 0.3989422804014327
SCALE = DH ** (-0.5)

ROW_OUT = 3456
ROW_FC1 = 4608
ROW_FC2 = 9216
ROW_VEC = 13824
QUARTER = 3466
PAD_Q = 3488
VEC_AT = ROW_VEC - 3 * QUARTER
SLOT = 3584
HALF = SLOT // 2
BLOCK = SLOT // 4
PAIR = 3 * D
LATE = 2 * PAIR + 64
EARLY_HALF = PAIR // 2
LATE_HALF = LATE // 2
VEC_IN_LATE = VEC_AT - (SLOT - LATE_HALF)

F32 = jnp.float32
BF16 = jnp.bfloat16


def dot_nn(a, b):
    return lax.dot_general(a, b, (((1,), (0,)), ((), ())), preferred_element_type=F32)


def dot_nt(a, b):
    return lax.dot_general(a, b, (((1,), (1,)), ((), ())), preferred_element_type=F32)


def dot_tn(a, b):
    return lax.dot_general(a, b, (((0,), (0,)), ((), ())), preferred_element_type=F32)


def row_of(vec, start, count):
    return jnp.concatenate([vec[start + i : start + i + 1] for i in range(count)], axis=1)


def norm(values):
    center = values - jnp.mean(values, -1, keepdims=True)
    inv = lax.rsqrt(jnp.mean(center * center, -1, keepdims=True) + EPSILON)
    return center * inv, inv


def norm_back(grad_norm, normed, inv):
    inner = jnp.mean(grad_norm * normed, -1, keepdims=True)
    return inv * (grad_norm - jnp.mean(grad_norm, -1, keepdims=True) - normed * inner)


def head_mean_matrix():
    r = lax.broadcasted_iota(jnp.int32, (256, 128), 0)
    c = lax.broadcasted_iota(jnp.int32, (256, 128), 1)
    return jnp.where((r % 128) // DH == c // DH, 1.0 / DH, 0.0).astype(BF16)


def head_mean(x, matrix):
    hi = x.astype(BF16)
    lo = (x - hi.astype(F32)).astype(BF16)
    return dot_nn(jnp.concatenate([hi, lo], axis=1), matrix)


def lane_head(rows, h):
    lane = lax.broadcasted_iota(jnp.int32, (rows, 128), 1)
    return (lane // DH) == h, lane - DH * (1 - h)


def spread(hi_of):
    hi = hi_of.astype(BF16)
    rest = hi_of - hi.astype(F32)
    mid = rest.astype(BF16)
    return hi, mid, (rest - mid.astype(F32)).astype(BF16)


def in_lanes(other, terms):
    out = jnp.where(other == 2, terms[2], BF16(0.0))
    return jnp.where(other == 0, terms[0], jnp.where(other == 1, terms[1], out))


def fetch(place, sources, window, dst, sem):
    for i, src in enumerate(sources):
        @pl.when(place == i)
        def _(src=src):
            pltpu.make_async_copy(src.at[window], dst, sem).start()


def arrive(src, window, dst, sem):
    pltpu.make_async_copy(src.at[window], dst, sem).wait()


def pair_gains(vec):
    gains = vec[15:16]
    return (
        jnp.concatenate([gains[:, :DH], gains[:, :DH]], axis=1),
        jnp.concatenate([gains[:, DH:], gains[:, DH:]], axis=1),
    )


def qkv_attend_kernel(
    t0, t1, t2, t3, vec_in, own, beside, w1_in, c1_in,
    act_ref, w2_ref, qx_ref, k_ref, v_ref, out_ref, nq_ref, iq_ref, nk_ref, ik_ref, vec_ref,
    raw, flat, q_s, sem,
):
    own_len = t0.shape[0]
    rows = 2 * own_len
    step = own_len
    place = lax.axis_index("group")
    q0_rows = pl.ds(0, ROW_OUT)
    fetch(place, (own, beside, w1_in, c1_in), q0_rows, raw, sem)
    vec = vec_in[...].astype(F32)[2:42]
    vec_ref[...] = vec
    gain_one, bias_one, bias_qkv = row_of(vec, 0, 3), row_of(vec, 3, 3), row_of(vec, 6, 9)
    gain_q, gain_k = pair_gains(vec)

    for i, ref in enumerate((t0, t1, t2, t3)):
        n, _ = norm(ref[...].astype(F32))
        act_ref[step * i : step * i + step, :] = (n * gain_one + bias_one).astype(BF16)

    arrive(own, q0_rows, raw, sem)
    flat[...] = raw[...].astype(F32)
    for j in range(9):
        p, t = j % 3, j // 3
        w2_ref[p, :, 128 * t : 128 * t + 128] = flat[pl.ds(j, D, stride=9), :].astype(BF16)
    matrix = head_mean_matrix()

    def heads(x, gain, n_ref, i_ref, p):
        c = x - head_mean(x, matrix)
        inv = lax.rsqrt(head_mean(c * c, matrix) + EPSILON)
        n = c * inv
        n_ref[p] = n
        i_ref[p] = inv
        return n * gain

    def bias(p, t):
        return bias_qkv[:, D * t + 128 * p : D * t + 128 * p + 128]

    for p in range(3):
        x = dot_nn(act_ref[...], w2_ref[p, :, 128:])
        y = heads(x[:, :128] + bias(p, 1), gain_k, nk_ref, ik_ref, p)
        k_ref[p] = y.astype(BF16)
        v_ref[p] = (x[:, 128:] + bias(p, 2)).astype(BF16)
        x = dot_nn(act_ref[0:rows, :], w2_ref[p, :, :128]) + bias(p, 0)
        q_s[p] = heads(x, gain_q, nq_ref, iq_ref, p).astype(BF16) * BF16(SCALE)

    def attend(p, c):
        q, k, v = q_s[p], k_ref[p], v_ref[p]
        parts = []
        for h in range(2):
            mine, _ = lane_head(2 * rows, h)
            own_l, other = lane_head(rows, h)
            qm = jnp.where(own_l, q, BF16(0.0))
            e = jnp.exp(dot_nt(qm, k)).astype(BF16)
            o = dot_nn(e, jnp.where(mine, v, BF16(1.0)))
            parts.append(o / pltpu.roll(o, DH, 1))
            qx_ref[p, h] = jnp.where(own_l, qm, in_lanes(other, spread(-jnp.log(o))))
        own_l, _ = lane_head(rows, 0)
        out_ref[p] = jnp.where(own_l, parts[0], parts[1])
        return c

    lax.fori_loop(0, 3, attend, 0)


OUT_HEAD = (4, 3, 3)
FC1_HEAD = tuple((2 * QUARTER - ROW_FC1 - j + 11) // 12 for j in range(12))
FC2_HEAD = (3 * QUARTER - ROW_FC2) // 3


def mlp_kernel(
    t0, t1, o_ref, cot0, cot1, own, beside, w1_in, c1_in, w2_in, c2_in,
    yk_ref, ys_ref, gmid_ref, gattn_ref, keep_ref, send_ref, wout_ref,
    raw, raw0, quarters, slots, wo_s, w1_s, w2_s, x_s, act_s, n_s, gn_s, y_s, db1_s, cot_s, sems,
):
    own_len = t0.shape[0]
    place = lax.axis_index("group")
    core = place % 2
    all_rows, tail = pl.ds(0, PAD_Q), pl.ds(ROW_OUT, 16)
    fetch(place, (own, beside, w1_in, c1_in), tail, raw0, sems.at[0])
    fetch(place, (beside, own, c2_in, w2_in), all_rows, raw.at[0], sems.at[1])
    fetch(place, (w1_in, c1_in, own, beside), all_rows, raw.at[1], sems.at[2])
    fetch(place, (c2_in, w2_in, beside, own), all_rows, raw.at[2], sems.at[3])
    x_s[0:own_len, :] = t0[...].astype(F32)
    x_s[own_len:, :] = t1[...].astype(F32)
    cot_s[0:own_len, :] = cot0[...]
    cot_s[own_len:, :] = cot1[...]
    attn = jnp.concatenate([o_ref[p].astype(BF16) for p in range(3)], axis=1)
    arrive(own, tail, raw0, sems.at[0])
    for i in range(3):
        arrive(own, all_rows, raw.at[i], sems.at[1 + i])
        quarters[i] = raw[i].astype(F32)
    first = raw0[...].astype(F32)
    vec = quarters[2, VEC_AT : VEC_AT + 40, :]
    bias_out, gain_two, bias_two = row_of(vec, 16, 3), row_of(vec, 19, 3), row_of(vec, 22, 3)
    bias_fc1, bias_fc2 = row_of(vec, 25, 12), row_of(vec, 37, 3)
    q1, q2, q3 = quarters.at[0], quarters.at[1], quarters.at[2]
    for j in range(3):
        n = OUT_HEAD[j]
        top = jnp.concatenate([first[3 * i + j : 3 * i + j + 1] for i in range(n)], axis=0)
        rest = q1[pl.ds(3 * n + j - 10, D - n, stride=3), :]
        wo_s[:, 128 * j : 128 * j + 128] = jnp.concatenate([top, rest], axis=0).astype(BF16)
        top = q2[pl.ds(ROW_FC2 - 2 * QUARTER + j, FC2_HEAD, stride=3), :]
        rest = q3[pl.ds(j, FF - FC2_HEAD, stride=3), :]
        w2_s[:, 128 * j : 128 * j + 128] = jnp.concatenate([top, rest], axis=0).astype(BF16)
    for j in range(12):
        n = FC1_HEAD[j]
        top = q1[pl.ds(ROW_FC1 - QUARTER + j, n, stride=12), :]
        rest = q2[pl.ds(ROW_FC1 - 2 * QUARTER + 12 * n + j, D - n, stride=12), :]
        w1_s[:, 128 * j : 128 * j + 128] = jnp.concatenate([top, rest], axis=0).astype(BF16)

    mid = x_s[...] + dot_nn(attn, wo_s[...]) + bias_out
    n, inv = norm(mid)
    n_s[...] = n
    act_s[...] = (n * gain_two + bias_two).astype(BF16)
    y_s[...] = mid + bias_fc2
    gn_s[...] = jnp.zeros_like(gn_s)
    width = 256
    for f in range(FF // width):
        at = f * width
        w1 = w1_s[:, at : at + width]
        w2 = w2_s[at : at + width, :]
        x = dot_nn(act_s[...], w1) + bias_fc1[:, at : at + width]
        phi = 0.5 * (1.0 + lax.erf(x * INV_ROOT_TWO))
        hid = (x * phi).astype(BF16)
        slope = phi + x * jnp.exp(-0.5 * x * x) * INV_ROOT_TAU
        gb = (dot_nt(cot_s[...], w2) * slope).astype(BF16)
        y_s[...] += dot_nn(hid, w2)
        gn_s[...] += dot_nt(gb, w1)
        dw2 = dot_tn(hid, cot_s[...])
        cut = min(max(FC2_HEAD - at, 0), width)
        for j in range(3):
            piece = dw2[:, 128 * j : 128 * j + 128]
            if cut > 0:
                slots[pl.ds(SLOT + ROW_FC2 - 2 * QUARTER + 3 * at + j, cut, stride=3), :] = piece[:cut]
            if cut < width:
                base = 2 * SLOT + 3 * (at + cut - FC2_HEAD) + j
                slots[pl.ds(base, width - cut, stride=3), :] = piece[cut:]
        dw1 = dot_tn(act_s[...], gb)
        for i in range(width // 128):
            j = at // 128 + i
            n1 = FC1_HEAD[j]
            piece = dw1[:, 128 * i : 128 * i + 128]
            slots[pl.ds(ROW_FC1 - QUARTER + j, n1, stride=12), :] = piece[:n1]
            base = SLOT + ROW_FC1 - 2 * QUARTER + 12 * n1 + j
            slots[pl.ds(base, D - n1, stride=12), :] = piece[n1:]
        db1_s[:, at : at + width] = jnp.sum(gb.astype(F32), 0, keepdims=True)
    yk_ref[...] = y_s[0:own_len, :].astype(BF16)
    ys_ref[...] = y_s[own_len:, :].astype(BF16)
    gn = gn_s[...]
    cot = cot_s[...].astype(F32)
    gmid = cot + norm_back(gn * gain_two, n_s[...], inv)
    gmid_ref[...] = gmid
    gproj = gmid.astype(BF16)
    gattn = dot_nt(gproj, wo_s[...]).astype(BF16)
    for p in range(3):
        gattn_ref[p] = gattn[:, 128 * p : 128 * p + 128]
    dwo = dot_tn(attn, gproj)
    for j in range(3):
        n0 = OUT_HEAD[j]
        piece = dwo[:, 128 * j : 128 * j + 128]
        slots[pl.ds(QUARTER + j, n0, stride=3), :] = piece[:n0]
        slots[pl.ds(3 * n0 + j - 10, D - n0, stride=3), :] = piece[n0:]
    slots[QUARTER + 10 : SLOT, :] = jnp.zeros((SLOT - QUARTER - 10, 128), F32)
    slots[SLOT + QUARTER : 2 * SLOT, :] = jnp.zeros((SLOT - QUARTER, 128), F32)
    slots[2 * SLOT + VEC_AT : 3 * SLOT, :] = jnp.zeros((SLOT - VEC_AT, 128), F32)

    def put(at, row):
        for i in range(row.shape[1] // 128):
            slots[2 * SLOT + VEC_AT + at + i : 2 * SLOT + VEC_AT + at + i + 1, :] = row[:, 128 * i : 128 * i + 128]

    put(16, jnp.sum(gproj.astype(F32), 0, keepdims=True))
    put(19, jnp.sum(gn * n_s[...], 0, keepdims=True))
    put(22, jnp.sum(gn, 0, keepdims=True))
    put(25, db1_s[...])
    put(37, jnp.sum(cot, 0, keepdims=True))
    wout_ref[0:10, :] = slots[QUARTER : QUARTER + 10, :].astype(BF16)
    wout_ref[10:, :] = jnp.zeros((54, 128), BF16)

    def deal(odd, even):
        for i in range(2):
            odd[i * SLOT : i * SLOT + SLOT, :] = slots[2 * i * SLOT : 2 * i * SLOT + SLOT, :].astype(BF16)
            at = SLOT + i * HALF
            even[i * SLOT : i * SLOT + HALF, :] = slots[at : at + HALF, :].astype(BF16)
            even[i * SLOT + HALF : i * SLOT + SLOT, :] = jnp.zeros((HALF, 128), BF16)

    @pl.when(core == 0)
    def _():
        deal(send_ref, keep_ref)

    @pl.when(core != 0)
    def _():
        deal(keep_ref, send_ref)


def pairs_back_kernel(
    act_ref, qx_ref, k_ref, v_ref, out_ref, nq_ref, iq_ref, nk_ref, ik_ref, vec_ref, ga_ref, *refs, pair,
):
    if pair == 0:
        _, _, g_ref, sums_ref, keep_any, send_any, part, sems = refs
    elif pair == 1:
        g_ref, sums_ref, part = refs
    else:
        (t0, t1, t2, t3, w2_ref, gmid_ref, wout_ref, g0_ref, g1_ref, sums0, sums1, part1_ref,
         g_ref, sums_ref, go_ref, gt_ref, keep_ref, send_ref, part, vrow) = refs
    core = lax.axis_index("group") % 2
    rows = ga_ref.shape[0]
    gain_q, gain_k = pair_gains(vec_ref[...])
    matrix = head_mean_matrix()
    k, v, ga = k_ref[...], v_ref[...], ga_ref[...]
    inner = -float(DH) * head_mean(ga.astype(F32) * out_ref[...], matrix)
    terms = spread(pltpu.roll(inner, DH, 1))
    gq_t = jnp.zeros((128, rows), F32)
    gk = jnp.zeros((2 * rows, 128), F32)
    gv = jnp.zeros((2 * rows, 128), F32)
    for h in range(2):
        mine, other_all = lane_head(2 * rows, h)
        own, other = lane_head(rows, h)
        ones = jnp.where((other_all >= 0) & (other_all <= 2), 1.0, 0.0).astype(BF16)
        qx = qx_ref[h]
        gax = jnp.where(own, ga, in_lanes(other, terms))
        prob = jnp.exp(dot_nt(jnp.where(mine, k, ones), qx))
        gprob = dot_nt(jnp.where(mine, v, ones), gax)
        gs = (prob * gprob).astype(BF16)
        gv = gv + dot_nn(prob.astype(BF16), jnp.where(own, ga, BF16(0.0)))
        gk = gk + dot_nn(gs, jnp.where(own, qx, BF16(0.0)))
        gq_t = gq_t + dot_tn(jnp.where(mine, k, BF16(0.0)), gs)
    gq = (gq_t.T * SCALE).astype(BF16).astype(F32)
    gk = gk.astype(BF16).astype(F32)

    def head_back(u, n, inv, gain):
        dn = u * gain
        return (inv * (dn - head_mean(dn, matrix) - n * head_mean(dn * n, matrix))).astype(BF16)

    def total(a):
        return jnp.sum(a, 0, keepdims=True)

    gq_b = head_back(gq, nq_ref[...], iq_ref[...], gain_q)
    gk_b = head_back(gk, nk_ref[...], ik_ref[...], gain_k)
    gv_b = gv.astype(BF16)
    g_ref[0:rows, 0:128] = gq_b
    g_ref[rows:, 0:128] = jnp.zeros((rows, 128), BF16)
    g_ref[:, 128:256] = gk_b
    g_ref[:, 256:384] = gv_b
    sums_ref[0:1, :] = total(gq_b.astype(F32))
    sums_ref[1:2, :] = total(gk_b.astype(F32))
    sums_ref[2:3, :] = total(gv_b.astype(F32))
    sums_ref[3:4, :] = total(gq * nq_ref[...])
    sums_ref[4:5, :] = total(gk * nk_ref[...])
    sums_ref[5:8, :] = jnp.zeros((3, 128), F32)
    dwq = dot_tn(act_ref[0:rows, :], gq_b).astype(BF16)
    dwkv = dot_tn(act_ref[...], g_ref[:, 128:384]).astype(BF16)
    part[0:D, :] = dwq
    part[D : 2 * D, :] = dwkv[:, :128]
    part[2 * D : PAIR, :] = dwkv[:, 128:]
    if pair == 0:
        def move(into):
            copies = [
                pltpu.make_async_copy(
                    part.at[pl.ds(h * EARLY_HALF, EARLY_HALF)],
                    into.at[pl.ds(h * SLOT + HALF, EARLY_HALF)], sems.at[h],
                )
                for h in range(2)
            ]
            for copy in copies:
                copy.start()
            for copy in copies:
                copy.wait()

        @pl.when(core == 0)
        def _():
            move(keep_any)

        @pl.when(core != 0)
        def _():
            move(send_any)
    if pair < 2:
        return
    own_len = t0.shape[0]
    gain_one = row_of(vec_ref[...], 0, 3)
    d_gain = jnp.zeros((1, D), F32)
    d_bias = jnp.zeros((1, D), F32)
    for i, ref in enumerate((t0, t1, t2, t3)):
        at = own_len * i
        cols = slice(0, D) if i < 2 else slice(128, D)
        u = sum(
            dot_nt(g[at : at + own_len, cols], w2_ref[p, :, cols])
            for p, g in enumerate((g0_ref, g1_ref, g_ref))
        )
        n, inv = norm(ref[...].astype(F32))
        d_gain = d_gain + total(u * n)
        d_bias = d_bias + total(u)
        back = norm_back(u * gain_one, n, inv)
        if i < 2:
            go_ref[at : at + own_len, :] = gmid_ref[at : at + own_len, :] + back
        else:
            gt_ref[at - rows : at - rows + own_len, :] = back.astype(BF16)
    for i in range(3):
        vrow[i : i + 1, :] = d_gain[:, 128 * i : 128 * i + 128]
        vrow[3 + i : 4 + i, :] = d_bias[:, 128 * i : 128 * i + 128]
    sums = (sums0[...], sums1[...], sums_ref[...])
    for p, s in enumerate(sums):
        for t in range(3):
            vrow[6 + 3 * t + p : 7 + 3 * t + p, :] = s[t : t + 1, :]
    dgq = sums[0][3:4, :] + sums[1][3:4, :] + sums[2][3:4, :]
    dgk = sums[0][4:5, :] + sums[1][4:5, :] + sums[2][4:5, :]
    low, _ = lane_head(1, 0)
    vrow[15:16, :] = jnp.where(low, dgq + pltpu.roll(dgq, DH, 1), dgk + pltpu.roll(dgk, DH, 1))

    def deal(matrix_to, vector_to):
        matrix_to[0:PAIR, :] = part1_ref[...]
        matrix_to[PAIR : 2 * PAIR, :] = part[...]
        matrix_to[2 * PAIR :, :] = wout_ref[...]
        vector_to[...] = jnp.zeros((LATE, 128), BF16)
        vector_to[VEC_IN_LATE - 2 : VEC_IN_LATE + 30, :] = jnp.concatenate(
            [jnp.zeros((2, 128), F32), vrow[...], jnp.zeros((14, 128), F32)], axis=0
        ).astype(BF16)

    @pl.when(core == 0)
    def _():
        deal(keep_ref, send_ref)

    @pl.when(core != 0)
    def _():
        deal(send_ref, keep_ref)


def finish_kernel(cat, got, out, slot, *, bits):
    place, rep = lax.axis_index("group"), lax.axis_index("replica")
    y = jnp.minimum(rep & bits[0], 1)
    t0, t1 = jnp.minimum(rep & bits[1], 1), jnp.minimum(rep & bits[-1], 1)
    t = jnp.where(place % 2 == 0, t0, t1)
    one, two = jnp.where(place % 2 == 0, 2, 1), jnp.where(place % 2 == 0, 1, 2)
    mine = 2 * y + t
    spots = (mine, mine ^ one, mine ^ two, 3 - mine)

    def blocks(into):
        for i in range(4):
            src = (cat, got)[i // 2]
            off = pl.multiple_of(spots[i] * BLOCK, 16)
            into[pl.ds(off, BLOCK), :] = src[(i % 2) * BLOCK : (i % 2) * BLOCK + BLOCK, :].astype(F32)

    @pl.when(place != 0)
    def _():
        blocks(out)

    @pl.when(place == 0)
    def _():
        blocks(slot)

        def rows(start, stop):
            late = start >= PAIR
            half, skip, base = (LATE_HALF, EARLY_HALF, PAIR) if late else (EARLY_HALF, 0, 0)
            pieces = []
            while start < stop:
                h = (start - base) // half
                end = min(stop, base + (h + 1) * half)
                row = h * HALF + skip + start - base - h * half
                pieces.append(slot[row : row + end - start, :])
                start = end
            return pieces[0] if len(pieces) == 1 else jnp.concatenate(pieces, axis=0)

        for p in range(3):
            for t in range(3):
                out[pl.ds(3 * t + p, D, stride=9), :] = rows(PAIR * p + D * t, PAIR * p + D * t + D)
        out[ROW_OUT : ROW_OUT + 10, :] = rows(3 * PAIR, 3 * PAIR + 10)


def shape(*dims, dtype=BF16):
    return jax.ShapeDtypeStruct(dims, dtype)


def vmem(*dims, dtype=BF16):
    return pltpu.VMEM(dims, dtype)


class Plan:
    def __init__(self, replicas):
        self.replicas = replicas
        self.bits = []
        while 2 ** len(self.bits) < replicas:
            self.bits.append(2 ** len(self.bits))
        self.thirds = (self.bits[1], self.bits[-1])
        self.rest = list(zip(self.bits[2:], self.bits[-2:0:-1]))

    def swap(self, a, dims, places=(0, 1, 2, 3)):
        pairs = []
        for rep in range(self.replicas):
            for place in places:
                dim = dims[place % 2]
                if dim is not None:
                    to = (rep, place ^ 2) if dim == "x" else (rep ^ dim, place)
                    pairs.append((place * self.replicas + rep, to[1] * self.replicas + to[0]))
        return lax.ppermute(a, ("group", "replica"), pairs)


def whole(a):
    return pl.BlockSpec(a.shape, lambda i, n=len(a.shape): (0,) * n)


ANY = pl.BlockSpec(memory_space=pl.ANY)


def call(kernel, args, outs, scratch=(), specs=None, out_specs=None, flops=0, aliases={}):
    specs = specs or [None] * len(args)
    out_specs = out_specs or [None] * len(outs)
    return pl.pallas_call(
        kernel,
        out_shape=outs,
        grid=(1,),
        in_specs=[s or whole(a) for s, a in zip(specs, args)],
        out_specs=tuple(s or whole(o) for s, o in zip(out_specs, outs)),
        scratch_shapes=list(scratch),
        cost_estimate=pl.CostEstimate(flops=flops, transcendentals=0, bytes_accessed=0) if flops else None,
        input_output_aliases=aliases,
    )(*args)


def per_device(tokens, cotangent, weight, momentum, average, rate, step, replicas):
    _, own_len, _ = tokens.shape
    rows = 2 * own_len
    x, c = lax.axis_index("group") // 2, lax.axis_index("group") % 2
    plan = Plan(replicas)

    place, rep = lax.axis_index("group"), lax.axis_index("replica")
    y = jnp.minimum(rep & plan.bits[0], 1)
    t = jnp.minimum(rep & jnp.where(c == 0, plan.thirds[0], plan.thirds[1]), 1)
    at_1 = [b * SLOT for b in (jnp.where(c == 0, y, x), jnp.where(c == 0, 1 - y, 1 - x))]
    at_3 = [jnp.where(c == 0, b * LATE_HALF, 0) for b in (y, 1 - y)]
    at_4 = [b * HALF for b in (jnp.where(c == 0, 1 - x, y), jnp.where(c == 0, x, 1 - y))]
    at_5 = [b * BLOCK for b in (t, 1 - t)]

    def move(a, pairs):
        return lax.ppermute(a, "group", pairs)

    def beside_of(a):
        return move(a, [(0, 1), (1, 0), (2, 3), (3, 2)])

    def over_x(a):
        return move(a, [(0, 2), (1, 3), (2, 0), (3, 1)])

    def pick(a, i):
        return lax.dynamic_index_in_dim(a, i, 0, keepdims=False)

    t1 = over_x(pick(tokens, 1 - x))
    t0 = pick(tokens, x)
    own = jnp.pad(weight.reshape(QUARTER, 128).astype(BF16), ((0, PAD_Q - QUARTER), (0, 0)))
    tail = own[VEC_AT - 2 : VEC_AT + 46]
    vec_x = move(tail, [(1, 3), (3, 1)])
    w1 = move(own, [(0, 2), (2, 0)])
    beside = beside_of(own)
    w2 = move(own, [(1, 3), (3, 1)])
    cot1 = over_x(pick(cotangent, 1 - x))
    cot0 = pick(cotangent, x)
    vec_b = jnp.where(place == 1, vec_x, tail)
    vec_b = jnp.where(c == 1, vec_b, beside_of(vec_b))
    t2, t3 = beside_of(t0), beside_of(t1)
    c1 = beside_of(w1)
    c2 = beside_of(w2)

    tok = [None] * 4
    act, w_cols, qx, k, v, out, nq, iq, nk, ik, vec = call(
        qkv_attend_kernel, (t0, t1, t2, t3, vec_b, own, beside, w1, c1),
        (
            shape(2 * rows, D), shape(3, D, D), shape(3, 2, rows, 128),
            shape(3, 2 * rows, 128), shape(3, 2 * rows, 128), shape(3, rows, 128, dtype=F32),
            shape(3, rows, 128, dtype=F32), shape(3, rows, 128, dtype=F32),
            shape(3, 2 * rows, 128, dtype=F32), shape(3, 2 * rows, 128, dtype=F32),
            shape(40, 128, dtype=F32),
        ),
        [
            vmem(ROW_OUT, 128), vmem(ROW_OUT, 128, dtype=F32), vmem(3, rows, 128),
            pltpu.SemaphoreType.DMA,
        ],
        specs=tok + [None] + [ANY] * 4, flops=10 ** 10,
    )
    yk, ys, gmid, gattn, keep, send, wout = call(
        mlp_kernel, (t0, t1, out, cot0, cot1, own, beside, w1, c1, w2, c2),
        (
            shape(own_len, D), shape(own_len, D), shape(rows, D, dtype=F32), shape(3, rows, 128),
            shape(2 * SLOT, 128), shape(2 * SLOT, 128), shape(64, 128),
        ),
        [
            vmem(3, PAD_Q, 128), vmem(16, 128), vmem(3, PAD_Q, 128, dtype=F32),
            vmem(3 * SLOT, 128, dtype=F32), vmem(D, D), vmem(D, FF), vmem(FF, D),
            vmem(rows, D, dtype=F32), vmem(rows, D), vmem(rows, D, dtype=F32),
            vmem(rows, D, dtype=F32), vmem(rows, D, dtype=F32), vmem(1, FF, dtype=F32), vmem(rows, D),
            pltpu.SemaphoreType.DMA((4,)),
        ],
        specs=[None] * 5 + [ANY] * 6, flops=10 ** 10,
    )

    def add(a, b):
        return (a.astype(F32) + b.astype(F32)).astype(BF16)

    def split(at, rows, total):
        return tuple(total(lambda a: lax.dynamic_slice_in_dim(a, at[i], rows, 0)) for i in range(2))

    def tie(a, b):
        return lax.optimization_barrier((a, b))

    def back(pair, first, extra=(), specs=(), outs=(), out_specs=(), scratch=(), aliases={}):
        def one(a):
            dims = tuple(a.shape[1:])
            return pl.BlockSpec((None,) + dims, lambda i, n=len(dims): (pair,) + (0,) * n)

        args = (act, qx, first, v, out, nq, iq, nk, ik, vec, gattn)
        in_specs = [None] + [one(a) for a in args[1:9]] + [None, one(gattn)] + list(specs)
        return call(
            lambda *refs: pairs_back_kernel(*refs, pair=pair), args + tuple(extra),
            (shape(2 * rows, D), shape(8, 128, dtype=F32)) + tuple(outs), scratch,
            specs=in_specs, out_specs=(None, None) + tuple(out_specs), flops=5 * 10 ** 9,
            aliases=aliases,
        )

    got_y = over_x(ys)
    g0, s0, keep, send = back(
        0, k, (keep, send), [ANY] * 2, (shape(2 * SLOT, 128), shape(2 * SLOT, 128)), [ANY] * 2,
        [vmem(PAIR, 128), pltpu.SemaphoreType.DMA((2,))], aliases={11: 2, 12: 3},
    )
    k1, send = tie(k, send)
    arrived = beside_of(send)
    g1, s1, part1 = back(1, k1, outs=(shape(PAIR, 128),), out_specs=(None,))
    kept, sent = split(at_1, SLOT, lambda cut: add(cut(keep), cut(arrived)))
    part1, sent = tie(part1, sent)
    got = plan.swap(sent, (plan.bits[0], "x"))
    extra = (t0, t1, t2, t3, w_cols, gmid, wout, g0, g1, s0, s1, part1)
    _, _, go, gt, keep_l, send_l = back(
        2, k, extra, [None] * 12,
        (shape(rows, D, dtype=F32), shape(rows, D), shape(LATE, 128), shape(LATE, 128)),
        [None] * 4, [vmem(PAIR, 128), vmem(16, 128, dtype=F32)],
    )
    arrived = beside_of(send_l)
    kept_l, sent = split(at_3, LATE_HALF, lambda cut: add(cut(keep_l), cut(arrived)))
    late = add(kept_l, plan.swap(sent, (plan.bits[0], "x")))
    late = jnp.where((c == 1) & (x == 0), BF16(0.0), late)

    def with_late(cut):
        below = jnp.where(c == 0, HALF + EARLY_HALF, SLOT - LATE_HALF)
        zeros = jnp.zeros((SLOT, 128), BF16)
        return add(add(cut(kept), cut(got)), cut(lax.dynamic_update_slice_in_dim(zeros, late, below, 0)))

    kept, sent = split(at_4, HALF, with_late)
    got = plan.swap(sent, ("x", plan.bits[0]))
    kept, sent = split(at_5, BLOCK, lambda cut: add(cut(kept), cut(got)))
    part = add(kept, plan.swap(sent, plan.thirds))
    for dims in plan.rest:
        part = add(part, plan.swap(part, dims))
    cat = jnp.concatenate([part, plan.swap(part, (plan.bits[0], plan.thirds[1]))])
    got = plan.swap(cat, (plan.thirds[0], plan.bits[0]))

    both = (go + beside_of(gt).astype(F32)).astype(BF16)
    got_g = over_x(both[own_len:])

    def given(kept, got):
        first = lax.broadcasted_iota(jnp.int32, tokens.shape, 0) == x
        return jnp.where(first, kept[None], got[None])

    out_tokens = given(yk, got_y)
    grad_tokens = given(both[:own_len], got_g)
    grad = call(
        lambda *refs: finish_kernel(*refs, bits=plan.bits), (cat, got),
        (shape(SLOT, 128, dtype=F32),), [vmem(SLOT, 128, dtype=F32)],
    )[0]
    grad = grad[:QUARTER].reshape(-1)
    momentum_new = MOMENT * momentum + grad
    weight_new = weight - rate[0] * (grad + MOMENT * momentum_new)
    step_value = step[0].astype(F32)
    decay = jnp.minimum(DECAY_MAX, (1.0 + step_value) / (10.0 + step_value))
    average_new = decay * average + (1.0 - decay) * weight_new
    return (
        out_tokens, grad_tokens, grad, momentum_new, average_new, weight_new, weight_new.astype(BF16),
    )


def solution(mesh):
    tok, flat = P("replica", "group", None), P("group")

    def body(*args):
        return per_device(*args, replicas=mesh.shape["replica"])

    return jax.shard_map(
        body,
        mesh=mesh,
        in_specs=(tok, tok, flat, flat, flat, P(), P()),
        out_specs=(tok, tok, flat, flat, flat, flat, flat),
        check_vma=False,
    )
```

time: 204 us -> 170 us (0.83)
  other arithmetic: 35.4 us -> 17.2 us
  waiting for transfers between devices: 80 us -> 62.2 us
  Pallas kernels: 43.9 us -> 54.5 us
  local copies, waits for them, and re-layouts: 8.55 us -> 3.22 us
  starting transfers between devices: 32.2 us -> 29.5 us
    select_n x13 -> x3, other arithmetic: 20.9 us -> 2.73 us  [the longest x1 2.11 us: given(): return jnp.where(first, kept[None], got[None])]
    ppermute x29 -> x23, waiting for transfers between devices: 80 us -> 62.2 us  [the longest x7 42.3 us: swap(): return lax.ppermute(a, ('group', 'replica'), pairs)]
    pallas_call x3 -> x6, Pallas kernels: 43.9 us -> 54.5 us  [call(): pl.pallas_call(kernel, out_shape=outs, grid=(1,), in_specs=[s or whole(a)...]
    convert_element_type x11 -> x7, other arithmetic: 2.38 us -> 5.37 us  [the longest x6 5.3 us: add(): return (a.astype(F32) + b.astype(F32)).astype(BF16)]
    ppermute x29 -> x23, starting transfers between devices: 32.2 us -> 29.5 us  [the longest x16 17.6 us: move(): return lax.ppermute(a, 'group', pairs)]
    dynamic_slice x8 -> x0, local copies, waits for them, and re-layouts: 2.7 us -> none  [reduce_all(): sent = lax.dynamic_slice_in_dim(part, (1 - side) * n, n, 0)]
    convert_element_type x1, other arithmetic: 7.15 us -> 4.59 us  [per_device(): weight_new.astype(BF16)]
  transfers between devices with their start and end apart: 29 -> 23, of which waited for: 18 -> 10; matrix products, arithmetic and copies ran while one was open for 9% -> 4% of each run, Pallas kernels for 9% -> 12%
where the time goes in v2:
time: 170 us; the launch traced here: 169 us
  waiting for transfers between devices  62.2 us (37%)
  Pallas kernels  54.5 us (32%)
  starting transfers between devices  29.5 us (17%)
  other arithmetic  17.2 us (10%)
  local copies, waits for them, and re-layouts  3.22 us (2%)
  between operations  2.33 us (1%)
    pallas_call x6, Pallas kernels, call(): pl.pallas_call(kernel, out_shape=outs, grid=(1,), in_specs=[s or whole(a)...  54.5 us
    ppermute x7, waiting for transfers between devices, swap(): return lax.ppermute(a, ('group', 'replica'), pairs)  42.3 us
    ppermute x16, waiting for transfers between devices, move(): return lax.ppermute(a, 'group', pairs)  20 us
    ppermute x16, starting transfers between devices, move(): return lax.ppermute(a, 'group', pairs)  17.6 us
    ppermute x7, starting transfers between devices, swap(): return lax.ppermute(a, ('group', 'replica'), pairs)  11.9 us
    convert_element_type x6, other arithmetic, add(): return (a.astype(F32) + b.astype(F32)).astype(BF16)  5.3 us
    convert_element_type x1, other arithmetic, per_device(): weight_new.astype(BF16)  4.59 us
  transfers between devices with their start and end apart: 23, of which 10 were waited for; matrix products, arithmetic and copies ran while one was open for 4% of the time, Pallas kernels for 12%

profile of v2, /device:TPU:0, one launch (start us, length us, event | category | flops | bytes accessed | tf_op | source)
XLA Modules:
  0.0 169.0 jit_solution(5027058258851058363)
XLA Ops:
  0.6 1.6 convert_bitcast_fusion
  2.2 0.0 copy-start.9
  2.2 0.0 copy-start.10
  2.2 0.1 pad.4.own
  2.3 0.0 copy-start.5
  2.3 5.0 %collective-permute-start.6 = (bf16[3488,128]{1,0:T(8,128)(2,1)S(1)}, bf16[3488,128]{1,0:T(8,128)(2,1)}, u32[]{:S(2)}, u32[]{:S(2)}) collective-permute-start(bf16[3488,128]{1,0:T(8,128)(2,1)S(1)} %pad.4.own), channel_id=1, source_target_pairs={{0,16},{16,0},{1,17},{17,1},{2,18},{18,2},{3,19},{19,3},{4,20},{20... | collective-permute-start | bytes 2678792 | tf_op jit(solution)/shard_map/ppermute | solution.py:546
  7.3 1.6 collective-permute-start.9
  8.9 18.4 %collective-permute-done.6.w1_in = bf16[3488,128]{1,0:T(8,128)(2,1)} collective-permute-done((bf16[3488,128]{1,0:T(8,128)(2,1)S(1)}, bf16[3488,128]{1,0:T(8,128)(2,1)}, u32[]{:S(2)}, u32[]{:S(2)}) %collective-permute-start.6) | collective-permute-done | bytes 892960 | tf_op jit(solution)/shard_map/ppermute | solution.py:546
  27.3 0.7 collective-permute-start.3
  28.1 2.4 %collective-permute-start = (bf16[256,384]{1,0:T(8,128)(2,1)S(1)}, bf16[256,384]{1,0:T(8,128)(2,1)S(1)}, u32[]{:S(2)}, u32[]{:S(2)}) collective-permute-start(bf16[256,384]{1,0:T(8,128)(2,1)S(1)} %get-tuple-element.85), channel_id=1, source_target_pairs={{0,16},{8,24},{16,0},{24,8},{1,17},{9,25},{17,1},{25,9},{2,18},{10... | collective-permute-start | bytes 589832 | tf_op jit(solution)/shard_map/ppermute | solution.py:546
  30.5 0.0 collective-permute-done.3
  30.5 2.8 %collective-permute-start.4 = (bf16[48,128]{1,0:T(8,128)(2,1)S(1)}, bf16[48,128]{1,0:T(8,128)(2,1)S(1)}, u32[]{:S(2)}, u32[]{:S(2)}) collective-permute-start(bf16[48,128]{1,0:T(8,128)(2,1)S(1)} %broadcast_select_fusion.2), channel_id=1, source_target_pairs={{0,8},{8,0},{16,24},{24,16},{1,9},{9,1},{17,25},{25,17},{2,10},{10... | collective-permute-start | bytes 36872 | tf_op jit(solution)/shard_map/ppermute | solution.py:546
  33.3 0.7 dynamic-slice_bitcast_fusion
  34.1 0.1 collective-permute-done.4
  34.2 0.3 collective-permute-start.1
  34.5 0.7 collective-permute-done.t1.refs_12_
  35.2 1.3 collective-permute-start.2
  36.5 0.6 broadcast_select_fusion.3.vec_in
  37.1 0.0 collective-permute-done.1.t2.refs_13_
  37.1 1.7 %collective-permute-start.8 = (bf16[256,384]{1,0:T(8,128)(2,1)S(1)}, bf16[256,384]{1,0:T(8,128)(2,1)S(1)}, u32[]{:S(2)}, u32[]{:S(2)}) collective-permute-start(bf16[256,384]{1,0:T(8,128)(2,1)S(1)} %get-tuple-element.83), channel_id=1, source_target_pairs={{0,16},{8,24},{16,0},{24,8},{1,17},{9,25},{17,1},{25,9},{2,18},{10... | collective-permute-start | bytes 589832 | tf_op jit(solution)/shard_map/ppermute | solution.py:546
  38.8 0.0 collective-permute-start.10
  38.8 0.0 collective-permute-done.2.t3.refs_14_
  38.9 0.6 copy-done.15
  39.5 14.2 %shard_map.126 = (bf16[1024,384]{1,0:T(8,128)(2,1)}, bf16[3,384,384]{2,1,0:T(8,128)(2,1)}, bf16[3,2,512,128]{3,2,1,0:T(8,128)(2,1)}, bf16[3,1024,128]{2,1,0:T(8,...) custom-call(bf16[256,384]{1,0:T(8,128)(2,1)} %copy-done.11, ...), custom_call_target="tpu_custom_call" | custom-call | flops 10000000000 | tf_op jit(solution)/shard_map/pallas_call | solution.py:519
  53.8 0.7 copy-done.16
  54.4 13.0 %shard_map.127 = (bf16[256,384]{1,0:T(8,128)(2,1)}, bf16[256,384]{1,0:T(8,128)(2,1)}, f32[512,384]{1,0:T(8,128)}, bf16[3,512,128]{2,1,0:T(8,128)(2,1)}, bf16[716...) custom-call(bf16[256,384]{1,0:T(8,128)(2,1)} %copy-done.11, bf16[256,384]{1,0:T(8,128)(2,1)} %copy-done.13, ...), custom_call_target="tpu_custom_call" | custom-call | flops 10000000000 | tf_op jit(solution)/shard_map/pallas_call | solution.py:519
  67.4 7.5 %shard_map.128 = (bf16[1024,384]{1,0:T(8,128)(2,1)}, f32[8,128]{1,0:T(8,128)}, bf16[7168,128]{1,0:T(8,128)(2,1)}, bf16[7168,128]{1,0:T(8,128)(2,1)}) custom-call(bf16[1024,384]{1,0:T(8,128)(2,1)} %get-tuple-element.43.refs_0_, bf16[3,2,512,128]{3,2,1,0:T(8,128)(2,1)} %get-tuple-element.44.refs_1_, ...), custom_call_target="tpu_custom_call", output_to_operand_aliasing={{2}: (11, {}), {3}: (12, {})} | custom-call | flops 5000000000 | tf_op jit(solution)/shard_map/pallas_call | solution.py:519
  74.9 0.6 collective-permute-start.12
  75.5 6.5 %shard_map.129 = (bf16[1024,384]{1,0:T(8,128)(2,1)}, f32[8,128]{1,0:T(8,128)}, bf16[1152,128]{1,0:T(8,128)(2,1)}) custom-call(bf16[1024,384]{1,0:T(8,128)(2,1)} %get-tuple-element.43.refs_0_, bf16[3,2,512,128]{3,2,1,0:T(8,128)(2,1)} %get-tuple-element.44.refs_1_, bf16[3,1024,128]{2,1,0:T(8,128)(2,1)} %get-tuple-element.60.refs_2_, ...), custom_call_target="tpu_custom_call" | custom-call | flops 5000000000 | tf_op jit(solution)/shard_map/pallas_call | solution.py:519
  82.0 2.9 %add_convert_fusion = (bf16[3584,128]{1,0:T(8,128)(2,1)S(1)}, bf16[3584,128]{1,0:T(8,128)(2,1)}) fusion(bf16[7168,128]{1,0:T(8,128)(2,1)S(1)} %collective-permute-done.12, s32[]{:T(128)S(6)} %select_n.125, bf16[7168,128]{1,0:T(8,128)(2,1)} %get-tuple-element.65, s32[]{:T(128)S(6)} %select_n.122), kind=kLoop, calls=%fused_computation | loop fusion | flops 3670016 | bytes 5505032 | tf_op jit(solution)/shard_map/convert_element_type | solution.py:606
  84.9 10.6 %shard_map.130 = (bf16[1024,384]{1,0:T(8,128)(2,1)}, f32[8,128]{1,0:T(8,128)}, f32[512,384]{1,0:T(8,128)}, bf16[512,384]{1,0:T(8,128)(2,1)}, bf16[2368,128]{1,0:T(8,128)(2,1)}, /*index=5*/bf16[2368,128]{1,0:T(8,128)(2,1)}) custom-call(bf16[1024,384]{1,0:T(8,128)(2,1)} %get-tuple-element.43.refs_0_, bf16[3,2,512,128]{3,2,1,0:T(8,128)(2,1)} %get-tuple-element.44.refs_1_, ...), custom_call_target="tpu_custom_call" | custom-call | flops 5000000000 | tf_op jit(solution)/shard_map/pallas_call | solution.py:519
  95.4 0.1 collective-permute-start.16
  95.6 1.6 collective-permute-start.15
  97.1 0.7 collective-permute-done.16
  97.9 1.9 %add_convert_fusion.8 = bf16[1184,128]{1,0:T(8,128)(2,1)} fusion(bf16[2368,128]{1,0:T(8,128)(2,1)} %collective-permute-done.16, s32[]{:T(128)S(6)} %select_n.132, bf16[2368,128]{1,0:T(8,128)(2,1)} %get-tuple-element.71), kind=kLoop, calls=%fused_computation.13 | loop fusion | flops 606208 | bytes 909316 | tf_op jit(solution)/shard_map/convert_element_type | solution.py:606
  99.7 1.5 collective-permute-start.17
  101.2 11.1 %collective-permute-done.17 = bf16[1184,128]{1,0:T(8,128)(2,1)} collective-permute-done((bf16[1184,128]{1,0:T(8,128)(2,1)}, bf16[1184,128]{1,0:T(8,128)(2,1)}, u32[]{:S(2)}, u32[]{:S(2)}) %collective-permute-start.17) | collective-permute-done | bytes 303136 | tf_op jit(solution)/shard_map/ppermute | solution.py:506
  112.3 0.1 broadcast.16
  112.5 1.2 fusion.1
  113.7 0.4 add_convert_fusion.4
  114.1 0.4 collective-permute-start.18
  114.5 8.1 %collective-permute-done.18 = bf16[1792,128]{1,0:T(8,128)(2,1)S(1)} collective-permute-done((bf16[1792,128]{1,0:T(8,128)(2,1)S(1)}, bf16[1792,128]{1,0:T(8,128)(2,1)S(1)}, u32[]{:S(2)}, u32[]{:S(2)}) %collective-permute-start.18) | collective-permute-done | bytes 458784 | tf_op jit(solution)/shard_map/ppermute | solution.py:506
  122.7 0.1 add_convert_fusion.12
  122.7 1.6 collective-permute-start.19
  124.4 0.5 collective-permute-start.11
  124.9 5.2 %collective-permute-done.19 = bf16[896,128]{1,0:T(8,128)(2,1)S(1)} collective-permute-done((bf16[896,128]{1,0:T(8,128)(2,1)S(1)}, bf16[896,128]{1,0:T(8,128)(2,1)S(1)}, u32[]{:S(2)}, u32[]{:S(2)}) %collective-permute-start.19) | collective-permute-done | bytes 229408 | tf_op jit(solution)/shard_map/ppermute | solution.py:506
  130.2 0.1 add_convert_fusion.11
  130.3 2.8 %collective-permute-start.20 = (bf16[896,128]{1,0:T(8,128)(2,1)S(1)}, bf16[896,128]{1,0:T(8,128)(2,1)S(1)}, u32[]{:S(2)}, u32[]{:S(2)}) collective-permute-start(bf16[896,128]{1,0:T(8,128)(2,1)S(1)} %add_convert_fusion.11), channel_id=1, source_target_pairs={{0,4},{8,10},{16,20},{24,26},{1,5},{9,11},{17,21},{25,27},{2,6},{1... | collective-permute-start | bytes 688136 | tf_op jit(solution)/shard_map/ppermute | solution.py:506
  133.0 0.1 add_convert_fusion.6
  133.1 9.5 %collective-permute-done.20 = bf16[896,128]{1,0:T(8,128)(2,1)S(1)} collective-permute-done((bf16[896,128]{1,0:T(8,128)(2,1)S(1)}, bf16[896,128]{1,0:T(8,128)(2,1)S(1)}, u32[]{:S(2)}, u32[]{:S(2)}) %collective-permute-start.20) | collective-permute-done | bytes 229408 | tf_op jit(solution)/shard_map/ppermute | solution.py:506
  142.6 0.1 add_convert_fusion.10
  142.7 1.6 collective-permute-start.21
  144.3 0.6 collective-permute-start.14
  144.9 5.4 %collective-permute-done.21 = bf16[896,128]{1,0:T(8,128)(2,1)S(1)} collective-permute-done((bf16[896,128]{1,0:T(8,128)(2,1)S(1)}, bf16[896,128]{1,0:T(8,128)(2,1)S(1)}, u32[]{:S(2)}, u32[]{:S(2)}) %collective-permute-start.21) | collective-permute-done | bytes 229408 | tf_op jit(solution)/shard_map/ppermute | solution.py:506
  150.3 0.0 copy-start.2
  150.3 2.3 %collective-permute-start.22 = (bf16[1792,128]{1,0:T(8,128)(2,1)S(1)}, bf16[1792,128]{1,0:T(8,128)(2,1)S(1)}, u32[]{:S(2)}, u32[]{:S(2)}) collective-permute-start(bf16[1792,128]{1,0:T(8,128)(2,1)S(1)} %pad_maximum_fusion.refs_0_), channel_id=1, source_target_pairs={{0,2},{8,9},{16,18},{24,25},{1,3},{9,8},{17,19},{25,24},{2,0},{10,... | collective-permute-start | bytes 1376264 | tf_op jit(solution)/shard_map/ppermute | solution.py:506
  154.0 0.0 copy-start.1
  154.1 2.1 %broadcast_select_fusion = (bf16[2,256,384]{2,1,0:T(8,128)(2,1)}, bf16[2,256,384]{2,1,0:T(8,128)(2,1)}) fusion(pred[2]{0:T(512)(128)(4,1)S(1)} %iota_compare_fusion, bf16[256,384]{1,0:T(8,128)(2,1)S(1)} %collective-permute-done.14, bf16[256,384]{1,0:T(8,128)(2,1)S(1)} %get-tuple-element.81, bf16[256,384]{1,0:T(8,128)(2,1)} %collective-permute-done.11, ...), kind=kLoop, calls=%fused_computation.20 | loop fusion | flops 393216 | bytes 1572866 | tf_op jit(solution)/shard_map/jit(_where)/select_n | solution.py:669
  156.2 2.9 %collective-permute-done.22.refs_1_ = bf16[1792,128]{1,0:T(8,128)(2,1)S(1)} collective-permute-done((bf16[1792,128]{1,0:T(8,128)(2,1)S(1)}, bf16[1792,128]{1,0:T(8,128)(2,1)S(1)}, u32[]{:S(2)}, u32[]{:S(2)}) %collective-permute-start.22) | collective-permute-done | bytes 458784 | tf_op jit(solution)/shard_map/ppermute | solution.py:506
  159.1 0.8 copy-done.8
  159.9 2.7 %shard_map.131 = f32[3584,128]{1,0:T(8,128)} custom-call(bf16[1792,128]{1,0:T(8,128)(2,1)} %copy-done.2, bf16[1792,128]{1,0:T(8,128)(2,1)} %copy-done.8), custom_call_target="tpu_custom_call" | custom-call | tf_op jit(solution)/shard_map/pallas_call | solution.py:519
  162.6 4.6 %fusion.2 = (bf16[443648]{0:T(1024)(128)(2,1)}, f32[443648]{0:T(1024)S(1)}, f32[443648]{0:T(1024)}, f32[443648]{0:T(1024)}) fusion(f32[443648]{0:T(1024)S(1)} %copy-done.1, f32[]{:T(128)} %bitcast.15, f32[443648]{0:T(1024)} %param.10, f32[3584,128]{1,0:T(8,128)} %shard_map.131), kind=kLoop, calls=%fused_computation.31 | loop fusion | flops 3105536 | bytes 11534852 | tf_op jit(solution)/shard_map/convert_element_type | solution.py:684
  167.2 1.7 multiply_add_fusion
  168.8 0.1 copy-done
  (44 shorter events, 0.2 us)
Async XLA Ops:
  2.2 25.8 %copy-start.9 = (bf16[2,256,384]{2,1,0:T(8,128)(2,1)S(1)}, bf16[2,256,384]{2,1,0:T(8,128)(2,1)}, u32[]{:S(2)}) copy-start(bf16[2,256,384]{2,1,0:T(8,128)(2,1)} %param.7) | copy-start | bytes 1179652
  2.2 31.1 %copy-start.10 = (bf16[2,256,384]{2,1,0:T(8,128)(2,1)S(1)}, bf16[2,256,384]{2,1,0:T(8,128)(2,1)}, u32[]{:S(2)}) copy-start(bf16[2,256,384]{2,1,0:T(8,128)(2,1)} %param.8) | copy-start | bytes 1179652
  2.3 36.6 %copy-start.5 = (bf16[3488,128]{1,0:T(8,128)(2,1)}, bf16[3488,128]{1,0:T(8,128)(2,1)S(1)}, u32[]{:S(2)}) copy-start(bf16[3488,128]{1,0:T(8,128)(2,1)S(1)} %pad.4.own) | copy-start | bytes 2678788
  2.3 25.0 %collective-permute-start.6 = (bf16[3488,128]{1,0:T(8,128)(2,1)S(1)}, bf16[3488,128]{1,0:T(8,128)(2,1)}, u32[]{:S(2)}, u32[]{:S(2)}) collective-permute-start(bf16[3488,128]{1,0:T(8,128)(2,1)S(1)} %pad.4.own), channel_id=1, source_target_pairs={{0,16},{16,0},{1,17},{17,1},{2,18},{18,2},{3,19},{19,3},{4,20},{20... | collective-permute-start | bytes 2678792 | tf_op jit(solution)/shard_map/ppermute | solution.py:546
  7.3 31.5 %collective-permute-start.9 = (bf16[3488,128]{1,0:T(8,128)(2,1)S(1)}, bf16[3488,128]{1,0:T(8,128)(2,1)}, u32[]{:S(2)}, u32[]{:S(2)}) collective-permute-start(bf16[3488,128]{1,0:T(8,128)(2,1)S(1)} %pad.4.own), channel_id=1, source_target_pairs={{8,24},{24,8},{9,25},{25,9},{10,26},{26,10},{11,27},{27,11},{12,28... | collective-permute-start | bytes 2678792 | tf_op jit(solution)/shard_map/ppermute | solution.py:546
  8.9 29.9 %collective-permute-start.5 = (bf16[3488,128]{1,0:T(8,128)(2,1)S(1)}, bf16[3488,128]{1,0:T(8,128)(2,1)}, u32[]{:S(2)}, u32[]{:S(2)}) collective-permute-start(bf16[3488,128]{1,0:T(8,128)(2,1)S(1)} %pad.4.own), channel_id=1, source_target_pairs={{0,8},{8,0},{16,24},{24,16},{1,9},{9,1},{17,25},{25,17},{2,10},{10... | collective-permute-start | bytes 2678792 | tf_op jit(solution)/shard_map/ppermute | solution.py:546
  27.3 11.5 %collective-permute-start.7 = (bf16[3488,128]{1,0:T(8,128)(2,1)}, bf16[3488,128]{1,0:T(8,128)(2,1)}, u32[]{:S(2)}, u32[]{:S(2)}) collective-permute-start(bf16[3488,128]{1,0:T(8,128)(2,1)} %collective-permute-done.6.w1_in), channel_id=1, source_target_pairs={{0,8},{8,0},{16,24},{24,16},{1,9},{9,1},{17,25},{25,17},{2,10},{10... | collective-permute-start | bytes 2678792 | tf_op jit(solution)/shard_map/ppermute | solution.py:546
  27.3 3.1 %collective-permute-start.3 = (bf16[48,128]{1,0:T(8,128)(2,1)S(1)}, bf16[48,128]{1,0:T(8,128)(2,1)S(1)}, u32[]{:S(2)}, u32[]{:S(2)}) collective-permute-start(bf16[48,128]{1,0:T(8,128)(2,1)S(1)} %pad_slice_fusion), channel_id=1, source_target_pairs={{8,24},{24,8},{9,25},{25,9},{10,26},{26,10},{11,27},{27,11},{12,28... | collective-permute-start | bytes 36872 | tf_op jit(solution)/shard_map/ppermute | solution.py:546
  28.1 10.8 %copy-start.11 = (bf16[256,384]{1,0:T(8,128)(2,1)}, bf16[256,384]{1,0:T(8,128)(2,1)S(1)}, u32[]{:S(2)}) copy-start(bf16[256,384]{1,0:T(8,128)(2,1)S(1)} %get-tuple-element.86.t0.refs_11_) | copy-start | bytes 589828
  28.1 7.1 %collective-permute-start = (bf16[256,384]{1,0:T(8,128)(2,1)S(1)}, bf16[256,384]{1,0:T(8,128)(2,1)S(1)}, u32[]{:S(2)}, u32[]{:S(2)}) collective-permute-start(bf16[256,384]{1,0:T(8,128)(2,1)S(1)} %get-tuple-element.85), channel_id=1, source_target_pairs={{0,16},{8,24},{16,0},{24,8},{1,17},{9,25},{17,1},{25,9},{2,18},{10... | collective-permute-start | bytes 589832 | tf_op jit(solution)/shard_map/ppermute | solution.py:546
  30.5 3.7 %collective-permute-start.4 = (bf16[48,128]{1,0:T(8,128)(2,1)S(1)}, bf16[48,128]{1,0:T(8,128)(2,1)S(1)}, u32[]{:S(2)}, u32[]{:S(2)}) collective-permute-start(bf16[48,128]{1,0:T(8,128)(2,1)S(1)} %broadcast_select_fusion.2), channel_id=1, source_target_pairs={{0,8},{8,0},{16,24},{24,16},{1,9},{9,1},{17,25},{25,17},{2,10},{10... | collective-permute-start | bytes 36872 | tf_op jit(solution)/shard_map/ppermute | solution.py:546
  34.2 2.9 %collective-permute-start.1 = (bf16[256,384]{1,0:T(8,128)(2,1)S(1)}, bf16[256,384]{1,0:T(8,128)(2,1)S(1)}, u32[]{:S(2)}, u32[]{:S(2)}) collective-permute-start(bf16[256,384]{1,0:T(8,128)(2,1)S(1)} %get-tuple-element.86.t0.refs_11_), channel_id=1, source_target_pairs={{0,8},{8,0},{16,24},{24,16},{1,9},{9,1},{17,25},{25,17},{2,10},{10... | collective-permute-start | bytes 589832 | tf_op jit(solution)/shard_map/ppermute | solution.py:546
  35.2 3.7 %copy-start.13 = (bf16[256,384]{1,0:T(8,128)(2,1)}, bf16[256,384]{1,0:T(8,128)(2,1)S(1)}, u32[]{:S(2)}) copy-start(bf16[256,384]{1,0:T(8,128)(2,1)S(1)} %collective-permute-done.t1.refs_12_) | copy-start | bytes 589828
  35.2 3.6 %collective-permute-start.2 = (bf16[256,384]{1,0:T(8,128)(2,1)S(1)}, bf16[256,384]{1,0:T(8,128)(2,1)S(1)}, u32[]{:S(2)}, u32[]{:S(2)}) collective-permute-start(bf16[256,384]{1,0:T(8,128)(2,1)S(1)} %collective-permute-done.t1.refs_12_), channel_id=1, source_target_pairs={{0,8},{8,0},{16,24},{24,16},{1,9},{9,1},{17,25},{25,17},{2,10},{10... | collective-permute-start | bytes 589832 | tf_op jit(solution)/shard_map/ppermute | solution.py:546
  37.1 1.8 %copy-start.14 = (bf16[256,384]{1,0:T(8,128)(2,1)}, bf16[256,384]{1,0:T(8,128)(2,1)S(1)}, u32[]{:S(2)}) copy-start(bf16[256,384]{1,0:T(8,128)(2,1)S(1)} %collective-permute-done.1.t2.refs_13_) | copy-start | bytes 589828
  37.1 16.7 %collective-permute-start.8 = (bf16[256,384]{1,0:T(8,128)(2,1)S(1)}, bf16[256,384]{1,0:T(8,128)(2,1)S(1)}, u32[]{:S(2)}, u32[]{:S(2)}) collective-permute-start(bf16[256,384]{1,0:T(8,128)(2,1)S(1)} %get-tuple-element.83), channel_id=1, source_target_pairs={{0,16},{8,24},{16,0},{24,8},{1,17},{9,25},{17,1},{25,9},{2,18},{10... | collective-permute-start | bytes 589832 | tf_op jit(solution)/shard_map/ppermute | solution.py:546
  38.8 15.0 %collective-permute-start.10 = (bf16[3488,128]{1,0:T(8,128)(2,1)}, bf16[3488,128]{1,0:T(8,128)(2,1)}, u32[]{:S(2)}, u32[]{:S(2)}) collective-permute-start(bf16[3488,128]{1,0:T(8,128)(2,1)} %collective-permute-done.9.w2_in), channel_id=1, source_target_pairs={{0,8},{8,0},{16,24},{24,16},{1,9},{9,1},{17,25},{25,17},{2,10},{10... | collective-permute-start | bytes 2678792 | tf_op jit(solution)/shard_map/ppermute | solution.py:546
  38.8 0.7 copy-start.15
  53.8 0.7 copy-start.16
  74.9 7.1 %collective-permute-start.12 = (bf16[7168,128]{1,0:T(8,128)(2,1)}, bf16[7168,128]{1,0:T(8,128)(2,1)S(1)}, u32[]{:S(2)}, u32[]{:S(2)}) collective-permute-start(bf16[7168,128]{1,0:T(8,128)(2,1)} %get-tuple-element.66), channel_id=1, source_target_pairs={{0,8},{8,0},{16,24},{24,16},{1,9},{9,1},{17,25},{25,17},{2,10},{10... | collective-permute-start | bytes 5505032 | tf_op jit(solution)/shard_map/ppermute | solution.py:546
  84.9 10.7 %copy-start.4 = (bf16[3584,128]{1,0:T(8,128)(2,1)S(1)}, bf16[3584,128]{1,0:T(8,128)(2,1)}, u32[]{:S(2)}) copy-start(bf16[3584,128]{1,0:T(8,128)(2,1)} %get-tuple-element.70) | copy-start | bytes 2752516
  95.4 17.0 %copy-start.7 = (bf16[2368,128]{1,0:T(8,128)(2,1)S(1)}, bf16[2368,128]{1,0:T(8,128)(2,1)}, u32[]{:S(2)}) copy-start(bf16[2368,128]{1,0:T(8,128)(2,1)} %get-tuple-element.71) | copy-start | bytes 1818628
  95.4 2.4 %collective-permute-start.16 = (bf16[2368,128]{1,0:T(8,128)(2,1)}, bf16[2368,128]{1,0:T(8,128)(2,1)}, u32[]{:S(2)}, u32[]{:S(2)}) collective-permute-start(bf16[2368,128]{1,0:T(8,128)(2,1)} %get-tuple-element.72), channel_id=1, source_target_pairs={{0,8},{8,0},{16,24},{24,16},{1,9},{9,1},{17,25},{25,17},{2,10},{10... | collective-permute-start | bytes 1818632 | tf_op jit(solution)/shard_map/ppermute | solution.py:546
  95.6 18.2 %collective-permute-start.15 = (bf16[3584,128]{1,0:T(8,128)(2,1)S(1)}, bf16[3584,128]{1,0:T(8,128)(2,1)S(1)}, u32[]{:S(2)}, u32[]{:S(2)}) collective-permute-start(bf16[3584,128]{1,0:T(8,128)(2,1)S(1)} %copy-done.4), channel_id=1, source_target_pairs={{0,1},{8,24},{16,17},{24,8},{1,0},{9,25},{17,16},{25,9},{2,3},{10,... | collective-permute-start | bytes 2752520 | tf_op jit(solution)/shard_map/ppermute | solution.py:506
  99.7 12.6 %collective-permute-start.17 = (bf16[1184,128]{1,0:T(8,128)(2,1)}, bf16[1184,128]{1,0:T(8,128)(2,1)}, u32[]{:S(2)}, u32[]{:S(2)}) collective-permute-start(bf16[1184,128]{1,0:T(8,128)(2,1)} %add_convert_fusion.8), channel_id=1, source_target_pairs={{0,1},{8,24},{16,17},{24,8},{1,0},{9,25},{17,16},{25,9},{2,3},{10,... | collective-permute-start | bytes 909320 | tf_op jit(solution)/shard_map/ppermute | solution.py:506
  113.7 19.3 %copy-start.6 = (f32[512,384]{1,0:T(8,128)S(1)}, f32[512,384]{1,0:T(8,128)}, u32[]{:S(2)}) copy-start(f32[512,384]{1,0:T(8,128)} %get-tuple-element.68) | copy-start | bytes 2359300
  114.1 8.5 %collective-permute-start.18 = (bf16[1792,128]{1,0:T(8,128)(2,1)S(1)}, bf16[1792,128]{1,0:T(8,128)(2,1)S(1)}, u32[]{:S(2)}, u32[]{:S(2)}) collective-permute-start(bf16[1792,128]{1,0:T(8,128)(2,1)S(1)} %get-tuple-element.80), channel_id=1, source_target_pairs={{0,16},{8,9},{16,0},{24,25},{1,17},{9,8},{17,1},{25,24},{2,18},{10... | collective-permute-start | bytes 1376264 | tf_op jit(solution)/shard_map/ppermute | solution.py:506
  122.7 7.4 %collective-permute-start.19 = (bf16[896,128]{1,0:T(8,128)(2,1)S(1)}, bf16[896,128]{1,0:T(8,128)(2,1)S(1)}, u32[]{:S(2)}, u32[]{:S(2)}) collective-permute-start(bf16[896,128]{1,0:T(8,128)(2,1)S(1)} %add_convert_fusion.12), channel_id=1, source_target_pairs={{0,2},{8,12},{16,18},{24,28},{1,3},{9,13},{17,19},{25,29},{2,0},{1... | collective-permute-start | bytes 688136 | tf_op jit(solution)/shard_map/ppermute | solution.py:506
  124.4 8.6 %collective-permute-start.13 = (bf16[512,384]{1,0:T(8,128)(2,1)}, bf16[512,384]{1,0:T(8,128)(2,1)S(1)}, u32[]{:S(2)}, u32[]{:S(2)}) collective-permute-start(bf16[512,384]{1,0:T(8,128)(2,1)} %get-tuple-element.69), channel_id=1, source_target_pairs={{0,8},{8,0},{16,24},{24,16},{1,9},{9,1},{17,25},{25,17},{2,10},{10... | collective-permute-start | bytes 1179656 | tf_op jit(solution)/shard_map/ppermute | solution.py:546
  124.4 29.7 %collective-permute-start.11 = (bf16[256,384]{1,0:T(8,128)(2,1)}, bf16[256,384]{1,0:T(8,128)(2,1)}, u32[]{:S(2)}, u32[]{:S(2)}) collective-permute-start(bf16[256,384]{1,0:T(8,128)(2,1)} %get-tuple-element.42), channel_id=1, source_target_pairs={{0,16},{8,24},{16,0},{24,8},{1,17},{9,25},{17,1},{25,9},{2,18},{10... | collective-permute-start | bytes 589832 | tf_op jit(solution)/shard_map/ppermute | solution.py:546
  130.3 12.3 %collective-permute-start.20 = (bf16[896,128]{1,0:T(8,128)(2,1)S(1)}, bf16[896,128]{1,0:T(8,128)(2,1)S(1)}, u32[]{:S(2)}, u32[]{:S(2)}) collective-permute-start(bf16[896,128]{1,0:T(8,128)(2,1)S(1)} %add_convert_fusion.11), channel_id=1, source_target_pairs={{0,4},{8,10},{16,20},{24,26},{1,5},{9,11},{17,21},{25,27},{2,6},{1... | collective-permute-start | bytes 688136 | tf_op jit(solution)/shard_map/ppermute | solution.py:506
  133.1 20.9 %copy-start.12 = (bf16[256,384]{1,0:T(8,128)(2,1)S(1)}, bf16[256,384]{1,0:T(8,128)(2,1)}, u32[]{:S(2)}) copy-start(bf16[256,384]{1,0:T(8,128)(2,1)} %get-tuple-element.41) | copy-start | bytes 589828
  142.7 7.6 %collective-permute-start.21 = (bf16[896,128]{1,0:T(8,128)(2,1)S(1)}, bf16[896,128]{1,0:T(8,128)(2,1)S(1)}, u32[]{:S(2)}, u32[]{:S(2)}) collective-permute-start(bf16[896,128]{1,0:T(8,128)(2,1)S(1)} %add_convert_fusion.10), channel_id=1, source_target_pairs={{0,1},{8,12},{16,17},{24,28},{1,0},{9,13},{17,16},{25,29},{2,3},{1... | collective-permute-start | bytes 688136 | tf_op jit(solution)/shard_map/ppermute | solution.py:506
  144.3 9.7 %collective-permute-start.14 = (bf16[256,384]{1,0:T(8,128)(2,1)S(1)}, bf16[256,384]{1,0:T(8,128)(2,1)S(1)}, u32[]{:S(2)}, u32[]{:S(2)}) collective-permute-start(bf16[256,384]{1,0:T(8,128)(2,1)S(1)} %get-tuple-element.82), channel_id=1, source_target_pairs={{0,16},{8,24},{16,0},{24,8},{1,17},{9,25},{17,1},{25,9},{2,18},{10... | collective-permute-start | bytes 589832 | tf_op jit(solution)/shard_map/ppermute | solution.py:546
  150.3 8.8 %copy-start.2 = (bf16[1792,128]{1,0:T(8,128)(2,1)}, bf16[1792,128]{1,0:T(8,128)(2,1)S(1)}, u32[]{:S(2)}) copy-start(bf16[1792,128]{1,0:T(8,128)(2,1)S(1)} %pad_maximum_fusion.refs_0_) | copy-start | bytes 1376260
  150.3 8.8 %collective-permute-start.22 = (bf16[1792,128]{1,0:T(8,128)(2,1)S(1)}, bf16[1792,128]{1,0:T(8,128)(2,1)S(1)}, u32[]{:S(2)}, u32[]{:S(2)}) collective-permute-start(bf16[1792,128]{1,0:T(8,128)(2,1)S(1)} %pad_maximum_fusion.refs_0_), channel_id=1, source_target_pairs={{0,2},{8,9},{16,18},{24,25},{1,3},{9,8},{17,19},{25,24},{2,0},{10,... | collective-permute-start | bytes 1376264 | tf_op jit(solution)/shard_map/ppermute | solution.py:506
  154.0 8.5 %copy-start.1 = (f32[443648]{0:T(1024)S(1)}, f32[443648]{0:T(1024)}, u32[]{:S(2)}) copy-start(f32[443648]{0:T(1024)} %param.9) | copy-start | bytes 5323780
  159.1 0.8 copy-start.8
  162.6 4.6 %copy-start.3 = (f32[443648]{0:T(1024)S(1)}, f32[443648]{0:T(1024)}, u32[]{:S(2)}) copy-start(f32[443648]{0:T(1024)} %param.11) | copy-start | bytes 5323780
  167.2 1.8 %copy-start = (f32[443648]{0:T(1024)}, f32[443648]{0:T(1024)S(1)}, u32[]{:S(2)}) copy-start(f32[443648]{0:T(1024)S(1)} %get-tuple-element.74) | copy-start | bytes 5323780
